TPU v7x, 256 devices: a whole 4x4x8 slice. The times are simulated.
256 devices in a mesh: ctx: 32 (over x, y, core), head: 8 (over z).
Axes of the slice: x: 4, y: 4, z: 8, core: 2. Of those that a mesh axis runs over, the one named last changes fastest.
Arguments:
- channels: bfloat16 [49152, 4096], P(('ctx', 'head')), may hold values from -6 to 6
- input_state_factors: bfloat16 [49152, 128], P(('ctx', 'head')), may hold values from -6 to 6
- c_coeffs: bfloat16 [49152, 128], P(('ctx', 'head')), may hold values from -6 to 6
- step_size_logits: bfloat16 [49152, 64], P(('ctx', 'head'))
- a_log: float32 [64], P('head')
- skip_gain: float32 [64], P('head'), may hold values from 0.5 to 1.5
- mix_gain: float32 [64, 3], P('head'), may hold values from -0.6 to 0.6
- offsets: int32 [384, 3], P('ctx'), may hold values from 1 to 6, as said below
- cotangent: bfloat16 [49152, 4096], P('ctx', 'head'), may hold values from -6 to 6
Outputs:
- mixed: bfloat16 [49152, 4096], P('ctx', 'head')
- grad_channels: bfloat16 [49152, 4096], P(('ctx', 'head'))
- grad_b: float32 [49152, 128], P(('ctx', 'head'))
- grad_c: float32 [49152, 128], P(('ctx', 'head'))
Inputs may be any that keep to these rules, and one draw needn't show every extreme that they name: Each block's 3 offsets are distinct; block b's neighbour in slot k is block b - offsets[b, k], and there is none where that index is negative.
All inputs are finite; a program needn't handle non-finite values.
Results may differ from a plain program's by a relative error of at most 0.0052.
Values may be sent and summed in bfloat16 or wider, within the bound.
No kernel may reach another device: no remote copies, remote signals or barrier semaphores. Data moves between devices by JAX's collectives and lax.ppermute only.
A program may use at most 128 MiB of HBM per device.

v0:
```python
import math

import jax
import jax.numpy as jnp
from jax import lax
from jax.sharding import PartitionSpec as P

P_SIZE = 64
N = 128
Q = 128


PRECISE = lax.Precision.HIGHEST


def entering(part, axis, combine, identity, reverse):
    count = lax.axis_size(axis)
    place = lax.axis_index(axis)
    ahead = count - 1 - place if reverse else place
    gathered = jax.tree.map(lambda a: lax.all_gather(a, axis), part)
    state = jax.tree.map(lambda a, e: jnp.zeros_like(a) + jnp.asarray(e, a.dtype), part, identity)

    def one(lap, state):
        source = count - 1 - lap if reverse else lap
        return combine(
            state, jax.tree.map(lambda a: lax.dynamic_index_in_dim(a, source, 0, False), gathered)
        )

    return lax.fori_loop(0, ahead, one, state)


def passed_along(value, axis, steps):
    count = lax.axis_size(axis)
    first, last = (max(0, -steps), min(count, count - steps))
    return lax.ppermute(value, axis, [(source, source + steps) for source in range(first, last)])


def link_states(earlier, latter):
    return (earlier[0] * latter[0], latter[0][:, None, None] * earlier[1] + latter[1])


def mix_blocks(own_rows, before, offset_rows, mixing):
    neighbour_count = before.shape[0]
    blocks_in = own_rows.shape[0]
    head_count = mixing.shape[0]
    row_width = own_rows.shape[-1]
    extended = jnp.concatenate([before, own_rows], axis=0)
    result = own_rows.astype(jnp.float32)
    for column in range(offset_rows.shape[1]):
        source = neighbour_count + jnp.arange(blocks_in, dtype=jnp.int32) - offset_rows[:, column]
        picked = jnp.take(extended, source, axis=0)
        weight = jnp.repeat(mixing[:, column], row_width // head_count)
        result = result + weight * picked.astype(jnp.float32)
    return result


def spread_terms(grad_rows, offset_rows, neighbour_count, mixing):
    blocks_in = grad_rows.shape[0]
    head_count = mixing.shape[0]
    row_width = grad_rows.shape[-1]
    places = jnp.arange(neighbour_count + blocks_in, dtype=jnp.int32)
    result = jnp.zeros((neighbour_count + blocks_in,) + grad_rows.shape[1:], jnp.float32)
    wide_rows = grad_rows.astype(jnp.float32)
    for column in range(offset_rows.shape[1]):
        target = neighbour_count + jnp.arange(blocks_in, dtype=jnp.int32) - offset_rows[:, column]
        select = (target[:, None] == places[None, :]).astype(jnp.float32)
        weight = jnp.repeat(mixing[:, column], row_width // head_count)
        result = result + jnp.einsum("be,bqf->eqf", select, weight * wide_rows, precision=PRECISE)
    return result


def body(
    channels,
    input_state_factors,
    c_coeffs,
    step_size_logits,
    a_log,
    skip_gain,
    mix_gain,
    offsets,
    cotangent,
):
    groups = lax.axis_size("head")
    tok_dev = channels.shape[0]
    ctx_tok = tok_dev * groups
    spans = ctx_tok // Q
    neighbour_count = spans // 2
    head_count = a_log.shape[0]
    row_width = head_count * P_SIZE
    in_scale = 1.0 / math.sqrt(N * ctx_tok * lax.axis_size("ctx"))
    chan_rows, dt_rows = (
        lax.all_to_all(channels, "head", split_axis=1, concat_axis=0, tiled=True),
        lax.all_to_all(step_size_logits, "head", split_axis=1, concat_axis=0, tiled=True),
    )
    b_rows, c_rows = (
        lax.all_gather(input_state_factors, "head", axis=0, tiled=True),
        lax.all_gather(c_coeffs, "head", axis=0, tiled=True),
    )
    log_decay = -jnp.exp(a_log)[None, :] * jax.nn.softplus(dt_rows.astype(jnp.float32))
    chan_four = chan_rows.reshape(spans, Q, head_count, P_SIZE)
    b_three = b_rows.reshape(spans, Q, N)
    c_three = c_rows.reshape(spans, Q, N)
    cum_log = jnp.cumsum(log_decay.reshape(spans, Q, head_count), axis=1)
    scores = (
        jnp.einsum("ctn,csn->cts", c_three, b_three, preferred_element_type=jnp.float32) * in_scale
    )
    causal = jnp.arange(Q)[:, None] >= jnp.arange(Q)[None, :]
    head_cum = jnp.transpose(cum_log, (0, 2, 1))
    log_gap = head_cum[:, :, :, None] - head_cum[:, :, None, :]
    decays = jnp.exp(jnp.where(causal, log_gap, -1e30))
    weights = (scores[:, None] * decays).astype(jnp.bfloat16)
    y_intra = jnp.einsum("chts,cshp->cthp", weights, chan_four, preferred_element_type=jnp.float32)
    end_decay = jnp.exp(cum_log[:, -1:, :] - cum_log)
    b_float = b_three.astype(jnp.float32)
    c_float = c_three.astype(jnp.float32)
    b_weighted = ((b_float * in_scale)[:, :, None, :] * end_decay[:, :, :, None]).astype(
        jnp.bfloat16
    )
    pieces = jnp.einsum(
        "cshn,cshp->chpn", b_weighted, chan_four, preferred_element_type=jnp.float32
    )
    totals = jnp.exp(cum_log[:, -1, :])

    def advance(state, element):
        factor, addend = element
        return (factor[:, None, None] * state + addend, state)

    zero_state = jnp.zeros((head_count, P_SIZE, N), jnp.float32)
    local_end, starts = lax.scan(advance, zero_state, (totals, pieces))
    inclusive = jnp.cumprod(totals, axis=0)
    before_span = jnp.concatenate([jnp.ones_like(inclusive[:1]), inclusive[:-1]], axis=0)
    dev_decay = inclusive[-1]
    identity = (jnp.ones_like(dev_decay), jnp.zeros_like(local_end))
    state_in = entering((dev_decay, local_end), "ctx", link_states, identity, False)[1]
    from_start = jnp.exp(cum_log)
    full_state = starts + before_span[:, :, None, None] * state_in[None]
    y_state = (
        jnp.einsum("cqn,chpn->cqhp", c_float, full_state, precision=PRECISE) * from_start[..., None]
    )
    outputs = y_intra + y_state + skip_gain[None, None, :, None] * chan_four.astype(jnp.float32)
    out_rows = outputs.astype(jnp.bfloat16).reshape(spans, Q, row_width)
    before = passed_along(out_rows[spans - neighbour_count :], "ctx", 1)
    mixed = (
        mix_blocks(out_rows, before, offsets, mix_gain)
        .astype(jnp.bfloat16)
        .reshape(ctx_tok, row_width)
    )
    mix_grad = cotangent.reshape(spans, Q, row_width)
    own_sums = spread_terms(mix_grad, offsets, neighbour_count, mix_gain)
    later_sums = passed_along(own_sums[:neighbour_count], "ctx", -1)
    padded = jnp.concatenate(
        [jnp.zeros((spans - neighbour_count,) + later_sums.shape[1:], jnp.float32), later_sums],
        axis=0,
    )
    grad_out = (mix_grad.astype(jnp.float32) + own_sums[neighbour_count:] + padded).astype(
        jnp.bfloat16
    )
    grad_four = grad_out.reshape(spans, Q, head_count, P_SIZE)
    grad_wide = grad_four.astype(jnp.float32)
    d_weights = jnp.einsum(
        "cthp,cshp->chts", grad_four, chan_four, preferred_element_type=jnp.float32
    )
    chan_grads = jnp.einsum(
        "chts,cthp->cshp", weights, grad_four, preferred_element_type=jnp.float32
    )
    grad_scores = jnp.sum(d_weights * decays, axis=1) * in_scale
    c_grads = jnp.einsum("cts,csn->ctn", grad_scores, b_float, precision=PRECISE)
    b_grads = jnp.einsum("cts,ctn->csn", grad_scores, c_float, precision=PRECISE)
    grad_scaled = grad_wide * from_start[..., None]
    grad_full = jnp.einsum("cqn,cqhp->chpn", c_float, grad_scaled, precision=PRECISE)
    c_grads = c_grads + jnp.einsum("cqhp,chpn->cqn", grad_scaled, full_state, precision=PRECISE)
    grad_in = jnp.einsum("ch,chpn->hpn", before_span, grad_full, precision=PRECISE)
    grad_end = entering((dev_decay, grad_in), "ctx", link_states, identity, True)[1]

    def backward_offset(grad_after, element):
        factor, grad_start = element
        return (grad_start + factor[:, None, None] * grad_after, grad_after)

    _, grad_pieces = lax.scan(backward_offset, grad_end, (totals, grad_full), reverse=True)
    chan_grads = chan_grads + jnp.einsum(
        "cshn,chpn->cshp", b_weighted.astype(jnp.float32), grad_pieces, precision=PRECISE
    )
    chan_scaled = chan_four.astype(jnp.float32) * end_decay[..., None]
    b_grads = (
        b_grads
        + jnp.einsum("cshp,chpn->csn", chan_scaled, grad_pieces, precision=PRECISE) * in_scale
    )
    chan_grads = chan_grads + skip_gain[None, None, :, None] * grad_wide
    grad_head = chan_grads.astype(jnp.bfloat16).reshape(ctx_tok, row_width)
    grad_channels = lax.all_to_all(grad_head, "head", split_axis=0, concat_axis=1, tiled=True)
    grad_b, grad_c = (
        lax.psum_scatter(b_grads.reshape(ctx_tok, N), "head", scatter_dimension=0, tiled=True),
        lax.psum_scatter(c_grads.reshape(ctx_tok, N), "head", scatter_dimension=0, tiled=True),
    )
    return (mixed, grad_channels, grad_b, grad_c)


def solution(mesh):
    placed = (
        P(("ctx", "head"), None),
        P(("ctx", "head"), None),
        P(("ctx", "head"), None),
        P(("ctx", "head"), None),
        P("head"),
        P("head"),
        P("head", None),
        P("ctx", None),
        P("ctx", "head"),
    )
    return jax.shard_map(
        body,
        mesh=mesh,
        in_specs=placed,
        out_specs=(
            P("ctx", "head"),
            P(("ctx", "head"), None),
            P(("ctx", "head"), None),
            P(("ctx", "head"), None),
        ),
        check_vma=False,
    )
```

profile of v0, /device:TPU:8, one launch (start us, length us, event | category | flops | bytes accessed | tf_op | source)
XLA Modules:
  0.0 523.7 jit_solution(9544333587375634351)
XLA Ops:
  7.2 8.5 %all-to-all-start = ((bf16[192,8,8]{0,2,1:T(8,128)(2,1)}), bf16[192,8,8]{0,2,1:T(8,128)(2,1)S(1)}, u32[]{:S(2)}, u32[]{:S(2)}) async-start(bf16[192,8,8]{0,2,1:T(8,128)(2,1)} %bitcast.183), calls=%async_computation | async-start | bytes 65536 | tf_op jit(solution)/shard_map/all_to_all | solution.py:93
  18.4 5.3 %all-to-all-done = bf16[192,8,8]{0,2,1:T(8,128)(2,1)S(1)} async-done(((bf16[192,8,8]{0,2,1:T(8,128)(2,1)}), bf16[192,8,8]{0,2,1:T(8,128)(2,1)S(1)}, u32[]{:S(2)}, u32[]{:S(2)}) %all-to-all-start) | async-done | bytes 24608 | tf_op jit(solution)/shard_map/all_to_all | solution.py:93
  28.0 55.0 %all_gather.23 = bf16[1536,128]{1,0:T(8,128)(2,1)S(1)} all-gather(bf16[192,128]{1,0:T(8,128)(2,1)S(1)} %copy-done.19), channel_id=1, replica_groups=mesh['ctx'=32,'head'=8] {'head'}, dimensions={0}, use_global_device_ids=true | all-gather | bytes 442368 | tf_op jit(solution)/shard_map/all_gather | solution.py:96
  89.9 5.1 reshape.159
  104.0 13.4 %while.58 = (s32[]{:T(128)}, f32[8,64,128]{2,1,0:T(8,128)S(1)}, f32[12,8,64,128]{3,2,1,0:T(8,128)S(1)}, f32[12,8]{1,0:T(8,128)S(1)}, f32[12,8,64,128]{3,2,1,0:T(8,128)}, /*index=5*/s32[]{:T(128)}, s32[]{:T(128)}) while((s32[]{:T(128)}, f32[8,64,128]{2,1,0:T(8,128)S(1)}, f32[12,8,64,128]{3,2,1,0:T(8,128)S(1)}, ...), condition=%wide.region_2.3_spmd.clone, body=%wide.region_1.2_spmd.clone.sunk | while | flops 262147 | bytes 1310924 | solution.py:129
  118.2 25.0 %all_gather.22 = bf16[1536,128]{1,0:T(8,128)(2,1)S(1)} all-gather(bf16[192,128]{1,0:T(8,128)(2,1)S(1)} %copy-done.20), channel_id=1, replica_groups=mesh['ctx'=32,'head'=8] {'head'}, dimensions={0}, use_global_device_ids=true | all-gather | bytes 442368 | tf_op jit(solution)/shard_map/all_gather | solution.py:97
  150.4 21.9 %all-gather.2 = f32[32,1,8]{2,1,0:T(1,128)S(1)} all-gather(f32[1,1,8]{2,1,0:T(1,128)S(1)} %bitcast.185), channel_id=1, replica_groups=mesh['ctx'=32,'head'=8] {'ctx'}, dimensions={0}, use_global_device_ids=true | all-gather | bytes 1056 | tf_op jit(solution)/shard_map/all_gather | solution.py:20
  217.0 5.2 %convert_multiply_fusion.2 = (f32[12,128,512]{2,1,0:T(8,128)S(1)}, f32[12,128,512]{2,1,0:T(8,128)S(1)}, f32[12,128,512]{2,1,0:T(8,128)S(1)}, bf16[12,128,512]{2,1,0:T(8,128)(2,1)}) fusion(bf16[12,128,512]{2,1,0:T(8,128)(2,1)} %bitcast.166, f32[512]{0:T(512)S(1)} %copy-done.21, f32[512]{0:T(512)} %mul.244, f32[512]{0:T(512)} %mul.247, ...), kind=kLoop, calls=%fused_computation.22 | loop fusion | flops 14155776 | bytes 18880548 | tf_op jit(solution)/shard_map/mul | solution.py:68
  226.8 6.3 %fusion.8 = f32[18,128,512]{2,0,1:T(8,128)} fusion(f32[12,128,512]{2,1,0:T(8,128)S(1)} %get-tuple-element.404, s32[12]{0:T(128)S(1)} %copy-done.24), kind=kOutput, calls=%fused_computation.31 | convolution fusion | flops 169869536 | bytes 7864368 | tf_op jit(solution)/shard_map/be,bqf->eqf/dot_general | solution.py:68
  233.1 6.7 %fusion.10 = f32[18,128,512]{2,0,1:T(8,128)} fusion(f32[12,128,512]{2,1,0:T(8,128)S(1)} %get-tuple-element.403, s32[12]{0:T(128)S(1)} %copy-done.23), kind=kOutput, calls=%fused_computation.33 | convolution fusion | flops 169869536 | bytes 7864368 | tf_op jit(solution)/shard_map/be,bqf->eqf/dot_general | solution.py:68
  239.8 14.3 %copy_add_fusion = f32[18,128,512]{2,1,0:T(8,128)} fusion(f32[18,128,512]{2,0,1:T(8,128)S(1)} %fusion.6, f32[18,128,512]{2,0,1:T(8,128)} %fusion.8, f32[18,128,512]{2,0,1:T(8,128)} %fusion.10), kind=kLoop, calls=%fused_computation.23 | loop fusion | flops 2359296 | bytes 18874368 | tf_op jit(solution)/shard_map/add | solution.py:68
  258.0 17.9 %collective-permute-done.1 = f32[6,128,512]{2,1,0:T(8,128)S(1)} collective-permute-done((f32[6,128,512]{2,1,0:T(8,128)S(1)}, f32[6,128,512]{2,1,0:T(8,128)S(1)}, u32[]{:S(2)}, u32[]{:S(2)}) %collective-permute-start.1) | collective-permute-done | bytes 1572896 | tf_op jit(solution)/shard_map/ppermute | solution.py:35
  282.5 4.8 fusion.13
  287.3 6.4 %fusion.4 = f32[8,1,64,128]{3,1,2,0:T(1,128)} fusion(f32[12,8,1,1]{0,2,3,1:T(1,128)S(1)} %bitcast.181, f32[12,8,64,128]{3,2,1,0:T(8,128)} %fusion.13), kind=kOutput, calls=%fused_computation.27 | convolution fusion | flops 9437184 | bytes 3408256 | tf_op jit(solution)/shard_map/ch,chpn->hpn/dot_general | solution.py:172
  299.9 6.5 %fusion.50 = f32[12,128,128]{2,1,0:T(8,128)} fusion(f32[12,128,128]{2,1,0:T(8,128)S(1)} %fusion.51, f32[12,8,64,128]{3,2,1,0:T(8,128)S(1)} %get-tuple-element.264, f32[8,64,128]{2,1,0:T(8,128)S(1)} %get-tuple-element.266, f32[12,8]{1,0:T(8,128)S(1)} %copy.200, bf16[12,128,8,64]{1,3,2,0:T(8,128)(2,1)S(1)} %bitcast.159, f32[12,128,8]{1,2,0:T(8,128)S(1)} %copy.201), kind=kOutput, calls=%fused_computation.84 | convolution fusion | flops 1211301888 | bytes 6603136 | tf_op jit(solution)/shard_map/cqhp,chpn->cqn/dot_general | solution.py:171
  306.4 76.3 %all-gather.8.cloned.1.call-done = f32[256,64,128]{2,1,0:T(8,128)} async-done(((f32[8,64,128]{2,1,0:T(8,128)}), f32[256,64,128]{2,1,0:T(8,128)}) %all-gather.8.cloned.1.call-update) | async-done | bytes 8388624 | tf_op jit(solution)/shard_map/all_gather | solution.py:20
  382.7 32.0 %while.56 = (s32[]{:T(128)}, f32[8,64,128]{2,1,0:T(8,128)S(1)}, s32[]{:T(128)}, f32[32,8]{1,0:T(8,128)S(1)}, f32[32,8,64,128]{3,2,1,0:T(8,128)}, /*index=5*/s32[]{:T(128)}, s32[]{:T(128)}, s32[]{:T(128)}, s32[]{:T(128)}) while((s32[]{:T(128)}, f32[8,64,128]{2,1,0:T(8,128)S(1)}, s32[]{:T(128)}, f32[32,8]{1,0:T(8,128)S(1)}, ...), condition=%wide.region_7.9_spmd, body=%wide.region_6.8_spmd.sunk | while | flops 131078 | bytes 786683 | solution.py:29
  415.1 21.6 %while.57 = (s32[]{:T(128)}, f32[8,64,128]{2,1,0:T(8,128)S(1)}, f32[12,8,64,128]{3,2,1,0:T(8,128)S(1)}, f32[12,8,64,128]{3,2,1,0:T(8,128)}, f32[12,8]{1,0:T(8,128)}, /*index=5*/s32[]{:T(128)}, s32[]{:T(128)}) while((s32[]{:T(128)}, f32[8,64,128]{2,1,0:T(8,128)S(1)}, f32[12,8,64,128]{3,2,1,0:T(8,128)S(1)}, f32[12,8,64,128]{3,2,1,0:T(8,128)}, ...), condition=%wide.region_9.11_spmd, body=%wide.region_8.10_spmd.sunk | while | flops 131075 | bytes 1310925 | solution.py:179
  436.7 8.0 %fusion.2 = f32[12,8,64,128]{3,2,1,0:T(8,128)S(1)} fusion(f32[12,8,64,128]{3,2,1,0:T(8,128)S(1)} %get-tuple-element.268, f32[12,128,8]{1,2,0:T(8,128)S(1)} %copy.197, f32[12,128,128]{2,1,0:T(8,128)} %copy-done.8), kind=kOutput, calls=%fused_computation.25 | convolution fusion | flops 1211105280 | bytes 7127040 | tf_op jit(solution)/shard_map/cshn,chpn->cshp/dot_general | solution.py:180
  453.4 5.4 %reshape.158 = bf16[8,192,512]{2,1,0:T(8,128)(2,1)} reshape(bf16[12,128,8,64]{3,2,1,0:T(8,128)(2,1)} %copy.228) | data formatting | bytes 3145728 | tf_op jit(solution)/shard_map/all_to_all | solution.py:190
  458.8 7.0 %all-to-all-start.2 = ((bf16[8,192,512]{2,1,0:T(8,128)(2,1)}), bf16[8,192,512]{2,1,0:T(8,128)(2,1)}, u32[]{:S(2)}, u32[]{:S(2)}) async-start(bf16[8,192,512]{2,1,0:T(8,128)(2,1)} %reshape.158), calls=%async_computation.2 | async-start | bytes 3145728 | tf_op jit(solution)/shard_map/all_to_all | solution.py:190
  466.1 6.8 %fusion.49 = f32[12,128,128]{2,1,0:T(8,128)S(1)} fusion(f32[12,8,64,128]{3,2,1,0:T(8,128)S(1)} %get-tuple-element.268, bf16[12,128,8,64]{1,3,2,0:T(8,128)(2,1)} %copy-done.3, f32[12,128,8]{1,2,0:T(8,128)S(1)} %copy.197), kind=kOutput, calls=%fused_computation.83 | convolution fusion | flops 1209729024 | bytes 5554176 | tf_op jit(solution)/shard_map/cshp,chpn->csn/dot_general | solution.py:186
  474.7 34.2 %all-to-all-done.2 = bf16[8,192,512]{2,1,0:T(8,128)(2,1)} async-done(((bf16[8,192,512]{2,1,0:T(8,128)(2,1)}), bf16[8,192,512]{2,1,0:T(8,128)(2,1)}, u32[]{:S(2)}, u32[]{:S(2)}) %all-to-all-start.2) | async-done | bytes 1572896 | tf_op jit(solution)/shard_map/all_to_all | solution.py:190
  511.6 5.3 %reduce-scatter.3.cloned.1.call-done = f32[192,128]{1,0:T(8,128)} async-done(((f32[1536,128]{1,0:T(8,128)}), f32[192,128]{1,0:T(8,128)}) %reduce-scatter.3.cloned.1.call-update) | async-done | bytes 98320 | tf_op jit(solution)/shard_map/reduce_scatter | solution.py:192
  (270 shorter events, 177.6 us)
Async XLA Ops:
  7.2 16.5 %all-to-all-start = ((bf16[192,8,8]{0,2,1:T(8,128)(2,1)}), bf16[192,8,8]{0,2,1:T(8,128)(2,1)S(1)}, u32[]{:S(2)}, u32[]{:S(2)}) async-start(bf16[192,8,8]{0,2,1:T(8,128)(2,1)} %bitcast.183), calls=%async_computation | async-start | bytes 65536 | tf_op jit(solution)/shard_map/all_to_all | solution.py:93
  15.6 12.4 %copy-start.19 = (bf16[192,128]{1,0:T(8,128)(2,1)S(1)}, bf16[192,128]{1,0:T(8,128)(2,1)}, u32[]{:S(2)}) copy-start(bf16[192,128]{1,0:T(8,128)(2,1)} %param.20) | copy-start | bytes 147460
  15.6 67.4 %copy-start.27 = (f32[8]{0:T(128)S(1)}, f32[8]{0:T(128)}, u32[]{:S(2)}) copy-start(f32[8]{0:T(128)} %param.23) | copy-start | bytes 100
  23.7 66.2 %all-to-all-start.1 = ((bf16[192,8,512]{2,0,1:T(8,128)(2,1)}), bf16[192,8,512]{2,0,1:T(8,128)(2,1)}, u32[]{:S(2)}, u32[]{:S(2)}) async-start(bf16[192,8,512]{2,0,1:T(8,128)(2,1)} %bitcast.135), calls=%async_computation.1 | async-start | bytes 3145728 | tf_op jit(solution)/shard_map/all_to_all | solution.py:92
  28.0 148.0 %all-gather.6.cloned.1.call-start = ((), (), s32[]{:S(2)}) async-start(), calls=%async_computation.7 | async-start | bytes 8650752 | tf_op jit(solution)/shard_map/all_gather | solution.py:20
  83.2 15.4 %copy-start.8 = (f32[12,128,128]{2,1,0:T(8,128)}, f32[12,128,128]{2,1,0:T(8,128)S(1)}, u32[]{:S(2)}) copy-start(f32[12,128,128]{2,1,0:T(8,128)S(1)} %convert_multiply_fusion.18) | copy-start | bytes 2359300
  103.9 14.2 %copy-start.20 = (bf16[192,128]{1,0:T(8,128)(2,1)S(1)}, bf16[192,128]{1,0:T(8,128)(2,1)}, u32[]{:S(2)}) copy-start(bf16[192,128]{1,0:T(8,128)(2,1)} %param.21) | copy-start | bytes 147460
  117.4 29.0 %copy-start.22 = (f32[12,8]{1,0:T(8,128)}, f32[12,8]{1,0:T(8,128)S(1)}, u32[]{:S(2)}) copy-start(f32[12,8]{1,0:T(8,128)S(1)} %get-tuple-element.665) | copy-start | bytes 1156
  118.1 264.6 %all-gather.8.cloned.1.call-start = ((), (), s32[]{:S(2)}) async-start(), calls=%async_computation.8 | async-start | bytes 8650752 | tf_op jit(solution)/shard_map/all_gather | solution.py:20
  185.6 6.7 %copy-start.26 = (f32[8,3]{0,1:T(4,128)S(1)}, f32[8,3]{0,1:T(4,128)}, u32[]{:S(2)}) copy-start(f32[8,3]{0,1:T(4,128)} %param.25) | copy-start | bytes 292
  188.9 14.0 %collective-permute-start = (bf16[6,128,512]{2,1,0:T(8,128)(2,1)}, bf16[6,128,512]{2,1,0:T(8,128)(2,1)}, u32[]{:S(2)}, u32[]{:S(2)}) collective-permute-start(bf16[6,128,512]{2,1,0:T(8,128)(2,1)} %copy.204), channel_id=1, source_target_pairs={{0,8},{8,16},{16,24},{24,32},{32,40},{40,48},{48,56},{56,64},{64,7... | collective-permute-start | bytes 2359304 | tf_op jit(solution)/shard_map/ppermute | solution.py:35
  209.7 7.3 %copy-start.21 = (f32[512]{0:T(512)S(1)}, f32[512]{0:T(512)}, u32[]{:S(2)}) copy-start(f32[512]{0:T(512)} %mul.241) | copy-start | bytes 6148
  226.8 6.3 %copy-start.23 = (s32[12]{0:T(128)S(1)}, s32[12]{0:T(128)}, u32[]{:S(2)}) copy-start(s32[12]{0:T(128)} %get-tuple-element.411) | copy-start | bytes 148
  254.1 21.9 %copy-start.9 = (bf16[1536,512]{1,0:T(8,128)(2,1)S(1)}, bf16[1536,512]{1,0:T(8,128)(2,1)}, u32[]{:S(2)}) copy-start(bf16[1536,512]{1,0:T(8,128)(2,1)} %param.27) | copy-start | bytes 4718596
  255.7 20.2 %collective-permute-start.1 = (f32[6,128,512]{2,1,0:T(8,128)S(1)}, f32[6,128,512]{2,1,0:T(8,128)S(1)}, u32[]{:S(2)}, u32[]{:S(2)}) collective-permute-start(f32[6,128,512]{2,1,0:T(8,128)S(1)} %slice.68), channel_id=1, source_target_pairs={{8,0},{16,8},{24,16},{32,24},{40,32},{48,40},{56,48},{64,56},{72,6... | collective-permute-start | bytes 4718600 | tf_op jit(solution)/shard_map/ppermute | solution.py:35
  293.7 217.9 %reduce-scatter.5.cloned.1.call-start = ((), (), s32[]{:S(2)}) async-start(), calls=%async_computation.6 | async-start | bytes 884736 | tf_op jit(solution)/shard_map/reduce_scatter | solution.py:193
  436.7 8.0 %copy-start.2 = (bf16[12,128,512]{1,2,0:T(8,128)(2,1)S(1)}, bf16[12,128,512]{1,2,0:T(8,128)(2,1)}, u32[]{:S(2)}) copy-start(bf16[12,128,512]{1,2,0:T(8,128)(2,1)} %copy.212) | copy-start | bytes 4718596
  436.7 8.0 %copy-start.16 = (f32[12,128,128]{2,1,0:T(8,128)S(1)}, f32[12,128,128]{2,1,0:T(8,128)}, u32[]{:S(2)}) copy-start(f32[12,128,128]{2,1,0:T(8,128)} %convolution_multiply_fusion) | copy-start | bytes 2359300
  436.7 8.0 %copy-start.18 = (f32[12,8,128]{2,1,0:T(8,128)S(1)}, f32[12,8,128]{2,1,0:T(8,128)}, u32[]{:S(2)}) copy-start(f32[12,8,128]{2,1,0:T(8,128)} %copy.190) | copy-start | bytes 147460
  436.7 8.0 %copy-start.29 = (f32[8]{0:T(128)S(1)}, f32[8]{0:T(128)}, u32[]{:S(2)}) copy-start(f32[8]{0:T(128)} %param.24) | copy-start | bytes 100
  458.8 50.0 %all-to-all-start.2 = ((bf16[8,192,512]{2,1,0:T(8,128)(2,1)}), bf16[8,192,512]{2,1,0:T(8,128)(2,1)}, u32[]{:S(2)}, u32[]{:S(2)}) async-start(bf16[8,192,512]{2,1,0:T(8,128)(2,1)} %reshape.158), calls=%async_computation.2 | async-start | bytes 3145728 | tf_op jit(solution)/shard_map/all_to_all | solution.py:190
  465.8 51.1 %reduce-scatter.3.cloned.1.call-start = ((), (), s32[]{:S(2)}) async-start(), calls=%async_computation.5 | async-start | bytes 884736 | tf_op jit(solution)/shard_map/reduce_scatter | solution.py:192
  466.1 6.8 %copy-start.6 = (bf16[1536,128]{1,0:T(8,128)(2,1)S(1)}, bf16[1536,128]{1,0:T(8,128)(2,1)}, u32[]{:S(2)}) copy-start(bf16[1536,128]{1,0:T(8,128)(2,1)} %copy-done.5) | copy-start | bytes 1179652
  466.1 6.8 %copy-start.14 = (f32[12,128,128]{2,1,0:T(8,128)S(1)}, f32[12,128,128]{2,1,0:T(8,128)}, u32[]{:S(2)}) copy-start(f32[12,128,128]{2,1,0:T(8,128)} %copy-done.13) | copy-start | bytes 2359300
  (15 other events, 42.1 us)
Sparse Core Ops, SparseCore 0:
  118.2 57.7 all-gather.5
  293.8 88.7 all-gather.7
  385.8 38.2 reduce-scatter.4
  474.8 42.0 reduce-scatter.2
where the time goes:
time: 533 us; the launch traced here: 524 us
  waiting for transfers between devices  143 us (27%)
  blocking collectives  102 us (19%)
  other arithmetic  92.3 us (17%)
  matrix products  73.5 us (14%)
  local copies, waits for them, and re-layouts  71 us (13%)
  starting transfers between devices  25.9 us (5%)
  between operations  14.5 us (3%)
    all_gather x2, waiting for transfers between devices, entering(): gathered = jax.tree.map(lambda a: lax.all_gather(a, axis), part)  79.9 us
    all_gather x1, blocking collectives, body(): lax.all_gather(input_state_factors, 'head', axis=0, tiled=True)  55 us
    all_to_all x1, waiting for transfers between devices, body(): lax.all_to_all(grad_head, 'head', split_axis=0, concat_axis=1, tiled=True)  34.2 us
    add x31, other arithmetic, link_states(): latter[0][:, None, None] * earlier[1] + latter[1]  32.9 us
    all_gather x1, blocking collectives, body(): lax.all_gather(c_coeffs, 'head', axis=0, tiled=True)  25 us
    all_gather x1, blocking collectives, entering(): gathered = jax.tree.map(lambda a: lax.all_gather(a, axis), part)  21.9 us
    ppermute x2, waiting for transfers between devices, passed_along(): lax.ppermute(value, axis, [(source, source + steps) for source in range(f...  17.9 us
    dot_general x3, matrix products, spread_terms(): jnp.einsum('be,bqf->eqf', select, weight * wide_rows, precision=PRECISE)  17.5 us
  transfers between devices with their start and end apart: 9, of which 6 were waited for; matrix products, arithmetic and copies ran while one was open for 24% of the time, Pallas kernels for 0%

commit v1 on v0

v1 whole, which is shorter than its diff:
```python
import functools
import math

import jax
import jax.numpy as jnp
from jax import lax
from jax.experimental import pallas as pl
from jax.experimental.pallas import tpu as pltpu
from jax.sharding import PartitionSpec as P


P_SIZE = 64
N = 128
Q = 128
PRECISE = lax.Precision.HIGHEST
F32 = jnp.float32
BF16 = jnp.bfloat16


def cost(us, moved=0):
    return pl.CostEstimate(flops=int(us * 5.0e8), bytes_accessed=int(moved), transcendentals=0)


def params(**kw):
    return pltpu.CompilerParams(dimension_semantics=("arbitrary",), **kw)


def nn(a, b):
    return lax.dot_general(a, b, (((1,), (0,)), ((), ())), preferred_element_type=F32)


def nt(a, b):
    return lax.dot_general(a, b, (((1,), (1,)), ((), ())), preferred_element_type=F32)


def tn(a, b):
    return lax.dot_general(a, b, (((0,), (0,)), ((), ())), preferred_element_type=F32)


def causal_mask():
    row = lax.broadcasted_iota(jnp.int32, (Q, Q), 0)
    col = lax.broadcasted_iota(jnp.int32, (Q, Q), 1)
    return row >= col


def left_half():
    return lax.broadcasted_iota(jnp.int32, (Q, 2 * P_SIZE), 1) < P_SIZE


def cumulative(ld):
    lower = jnp.where(causal_mask(), 1.0, 0.0).astype(F32)
    dims = (((1,), (1,)), ((), ()))
    rows = lax.dot_general(ld, lower, dims, precision=PRECISE, preferred_element_type=F32)
    cols = lax.dot_general(lower, ld, dims, precision=PRECISE, preferred_element_type=F32)
    return rows, cols


def lane_fill(cols, lane):
    return jnp.broadcast_to(cols[:, lane : lane + 1], (Q, 2 * P_SIZE))


def spread_heads(cols, heads):
    mask = left_half()
    return jnp.concatenate(
        [
            jnp.where(mask, lane_fill(cols, 2 * pair), lane_fill(cols, 2 * pair + 1))
            for pair in range(heads // 2)
        ],
        axis=1,
    )


def pack_kernel(b_ref, c_ref, dt_ref, out_ref):
    tokens = b_ref.shape[0]
    for j in range(out_ref.shape[0]):
        out_ref[j, :tokens, :N] = b_ref[...]
        out_ref[j, :tokens, N:] = c_ref[...]
        out_ref[j, tokens:, :] = dt_ref[j]


def split_kernel(me_ref, in_ref, *out_refs):
    count = len(out_refs)
    width = out_refs[0].shape[1]
    for d, out_ref in enumerate(out_refs):
        target = lax.rem(me_ref[0] + d, count)
        out_ref[...] = in_ref[:, pl.ds(pl.multiple_of(target * width, width), width)]


def gather_copies(sources, places, ext, sems):
    copies = []
    place = 0
    for number, (ref, (start, length)) in enumerate(zip(sources, places)):
        copies.append(
            pltpu.make_async_copy(
                ref.at[pl.ds(start, length)], ext.at[pl.ds(place, length)], sems.at[number]
            )
        )
        place += length
    for copy in copies:
        copy.start()
    for copy in copies:
        copy.wait()


def mix_back_kernel(places, coef_ref, *refs):
    out_ref, ext, sems = refs[-3], refs[-2], refs[-1]
    i = pl.program_id(0)
    steps = out_ref.shape[0]

    @pl.when(i == 0)
    def _():
        gather_copies(refs[:-3], places, ext, sems)

    for u in range(steps):
        acc = ext[steps * i + u].astype(F32)
        for d in range(1, 7):
            acc = acc + coef_ref[u, d - 1 : d, :] * ext[steps * i + u + d].astype(F32)
        out_ref[u] = acc.astype(BF16)


def mix_fore_kernel(places, first, offset_ref, gain_ref, *refs):
    out_ref, ext, sems = refs[-3], refs[-2], refs[-1]
    i = pl.program_id(0)
    steps = out_ref.shape[0]

    @pl.when(i == 0)
    def _():
        gather_copies(refs[: len(places)], places, ext, sems)

    for u in range(steps):
        block = steps * i + u
        acc = ext[6 + block].astype(F32)
        for k in range(offset_ref.shape[1]):
            picked = ext[6 + block - offset_ref[first + block, k]]
            acc = acc + gain_ref[k : k + 1, :] * picked.astype(F32)
        out_ref[u] = acc.astype(BF16)


def mix(kernel, heads, specs, sources, places, steps, first, count, total, into=None):
    width = sources[0].shape[-1]
    args = list(heads) + list(sources) + ([] if into is None else [into])
    return pl.pallas_call(
        kernel,
        grid=(count // steps,),
        in_specs=list(specs) + [pl.BlockSpec(memory_space=pl.ANY)] * (len(args) - len(heads)),
        out_specs=pl.BlockSpec((steps, Q, width), lambda i: (i + first // steps, 0, 0)),
        out_shape=jax.ShapeDtypeStruct((total, Q, width), BF16),
        scratch_shapes=[
            pltpu.VMEM((sum(length for _, length in places), Q, width), BF16),
            pltpu.SemaphoreType.DMA((len(places),)),
        ],
        input_output_aliases={} if into is None else {len(args) - 1: 0},
        compiler_params=params(),
        cost_estimate=cost(0.5 * count),
    )(*args)


def put_pieces(out_ref, state, decay=None):
    pieces = out_ref.shape[0]
    rows = state.shape[0] // pieces
    width = state.shape[1]
    for k in range(pieces):
        out_ref[k, :, :width] = state[k * rows : (k + 1) * rows]
        if decay is not None:
            out_ref[k, :, width:] = decay


def fold_row(row, rows):
    part = row.shape[1] // rows
    return jnp.concatenate([row[:, r * part : (r + 1) * part] for r in range(rows)], axis=0)


def unfold_row(block):
    return jnp.concatenate([block[r : r + 1] for r in range(block.shape[0])], axis=1)


def take_pieces(ref):
    return jnp.concatenate([ref[k] for k in range(ref.shape[0])], axis=0)


def token_rows(ref):
    used = 3 * Q // 2
    return jnp.concatenate([ref[0, :used], ref[1, :used]], axis=0)


def back_state_kernel(ld_ref, g_ref, c_ref, full_ref, cum_ref, row_ref, out_ref, state, total):
    heads = ld_ref.shape[0]
    i = pl.program_id(0)

    @pl.when(i == 0)
    def _():
        state[...] = jnp.zeros_like(state)
        total[...] = jnp.zeros_like(total)

    all_c = token_rows(c_ref)
    fulls = []
    lasts = []
    for u in range(g_ref.shape[0]):
        part = slice(u * Q, (u + 1) * Q)
        rows, cols = cumulative(ld_ref[:, part])
        row_ref[:, part] = rows
        cum = spread_heads(cols, heads)
        cum_ref[u] = cum
        scaled = (g_ref[u].astype(F32) * jnp.exp(cum)).astype(BF16)
        full = tn(all_c[part], scaled)
        full_ref[u] = full
        fulls.append(full)
        lasts.append(cum[Q - 1 : Q, :])
    now = state[...]
    for full, last in zip(fulls[::-1], lasts[::-1]):
        now = jnp.exp(last) * now + full
    state[...] = now
    total[...] = total[...] + sum(lasts)

    @pl.when(i == pl.num_programs(0) - 1)
    def _():
        put_pieces(out_ref, state[...], fold_row(jnp.exp(total[...]), out_ref.shape[1]))


def fore_state_kernel(in_scale, me_ref, cum_ref, b_ref, *refs):
    piece_ref, x_ref, out_ref, x_all, state, sems = refs[-6:]
    parts = refs[:-6]
    count = len(parts)
    i = pl.program_id(0)

    @pl.when(i == 0)
    def _():
        copies = []
        for d, part in enumerate(parts):
            source = lax.rem(me_ref[0] + count - d, count)
            copies.append(pltpu.make_async_copy(part, x_all.at[source], sems.at[d]))
        for copy in copies:
            copy.start()
        state[...] = jnp.zeros_like(state)
        for copy in copies:
            copy.wait()

    all_b = token_rows(b_ref)
    all_x = jnp.concatenate([x_all[2 * i], x_all[2 * i + 1]], axis=0)
    pieces = []
    lasts = []
    for u in range(x_ref.shape[0]):
        part = slice(u * Q, (u + 1) * Q)
        last = cum_ref[u, Q - 1 : Q, :]
        x = all_x[part]
        x_ref[u] = x
        scaled = (x.astype(F32) * jnp.exp(last - cum_ref[u])).astype(BF16)
        piece = tn(all_b[part], scaled) * in_scale
        piece_ref[u] = piece
        pieces.append(piece)
        lasts.append(last)
    now = state[...]
    for piece, last in zip(pieces, lasts):
        now = jnp.exp(last) * now + piece
    state[...] = now

    @pl.when(i == pl.num_programs(0) - 1)
    def _():
        put_pieces(out_ref, now)


def scan_kernel(reverse, decay_ref, in_ref, out_ref):
    count, rows, width = out_ref.shape
    state = jnp.zeros((rows, width), F32)
    for lap in range(count):
        source = count - 1 - lap if reverse else lap
        out_ref[source] = state
        decay = unfold_row(decay_ref[source, :, width:])
        state = decay * state + in_ref[source, :, :width]


def span_kernel(
    in_scale,
    me_ref,
    row_ref,
    cum_ref,
    x_ref,
    g_ref,
    b_ref,
    c_ref,
    full_ref,
    skip_ref,
    end_ref,
    *refs,
):
    y_ref, cg_ref = refs[:2]
    grad_refs = refs[2:-3]
    grads, state, sems = refs[-3:]
    heads = row_ref.shape[0]
    i = pl.program_id(0)
    count = len(grad_refs)
    tokens = grads.shape[1]
    group = pl.num_programs(0) - 1 - i
    slots = [lax.rem(2 * group + k + count - me_ref[0], count) for k in range(2)]

    def put_grad(u, lanes, value):
        start = u * Q
        while start < (u + 1) * Q:
            place = start // tokens
            stop = min((u + 1) * Q, (place + 1) * tokens)
            rows = slice(start - place * tokens, stop - place * tokens)
            grads[slots[place], rows, lanes] = value[start - u * Q : stop - u * Q]
            start = stop

    @pl.when(i == 0)
    def _():
        state[...] = take_pieces(end_ref)

    causal = causal_mask()
    mask = left_half()
    all_b = token_rows(b_ref)
    all_c = token_rows(c_ref)
    for u in range(x_ref.shape[0] - 1, -1, -1):
        part = slice(u * Q, (u + 1) * Q)
        b = all_b[part]
        c = all_c[part]
        scores = nt(c, b) * in_scale
        after = state[...]
        after_low = after.astype(BF16)
        inter = nn(b, after_low) * in_scale
        grad_scores = jnp.zeros((Q, Q), F32)
        x_ends = []
        for pair in range(heads // 2):
            lanes = slice(pair * 2 * P_SIZE, (pair + 1) * 2 * P_SIZE)
            x = x_ref[u, :, lanes]
            g = g_ref[u, :, lanes]
            zero = jnp.zeros_like(x)
            cum = cum_ref[u, :, lanes]
            gap0 = lane_fill(cum, 0) - row_ref[2 * pair : 2 * pair + 1, part]
            gap1 = lane_fill(cum, P_SIZE) - row_ref[2 * pair + 1 : 2 * pair + 2, part]
            decay0 = jnp.exp(jnp.where(causal, gap0, -1e30))
            decay1 = jnp.exp(jnp.where(causal, gap1, -1e30))
            weight0 = (scores * decay0).astype(BF16)
            weight1 = (scores * decay1).astype(BF16)
            x_two = jnp.concatenate([jnp.where(mask, x, zero), jnp.where(mask, zero, x)], axis=0)
            g_two = jnp.concatenate([jnp.where(mask, g, zero), jnp.where(mask, zero, g)], axis=0)
            skip = skip_ref[0:1, lanes]
            xf = x.astype(F32)
            y_ref[u, :, lanes] = (
                nn(jnp.concatenate([weight0, weight1], axis=1), x_two) + skip * xf
            )
            d_weights = nt(g_two, x)
            grad_scores = grad_scores + d_weights[:Q] * decay0 + d_weights[Q:] * decay1
            local = tn(jnp.concatenate([weight0, weight1], axis=0), g_two)
            end_decay = jnp.exp(cum[Q - 1 : Q, :] - cum)
            grad = local + end_decay * inter[:, lanes] + skip * g.astype(F32)
            put_grad(u, lanes, grad.astype(BF16))
            x_ends.append((xf * end_decay).astype(BF16))
        narrow = (grad_scores * in_scale).astype(BF16)
        b_sum = nt(jnp.concatenate(x_ends, axis=1), after_low) * in_scale
        put_grad(u, slice(heads * P_SIZE, None), (b_sum + tn(narrow, c)).astype(BF16))
        cg_ref[u] = nn(narrow, b)
        state[...] = jnp.exp(cum_ref[u, Q - 1 : Q, :]) * after + full_ref[u]

    @pl.when(i == pl.num_programs(0) - 1)
    def _():
        copies = [
            pltpu.make_async_copy(grads.at[d], ref, sems.at[d]) for d, ref in enumerate(grad_refs)
        ]
        for copy in copies:
            copy.start()
        for copy in copies:
            copy.wait()


def output_kernel(
    cum_ref, g_ref, c_ref, y_ref, cg_ref, piece_ref, start_ref, out_ref, c_out_ref, state
):
    @pl.when(pl.program_id(0) == 0)
    def _():
        state[...] = take_pieces(start_ref)

    all_c = token_rows(c_ref)
    now = state[...]
    for u in range(g_ref.shape[0]):
        from_start = jnp.exp(cum_ref[u])
        low = now.astype(BF16)
        out_ref[u] = (y_ref[u] + nn(all_c[u * Q : (u + 1) * Q], low) * from_start).astype(BF16)
        scaled = (g_ref[u].astype(F32) * from_start).astype(BF16)
        c_out_ref[u] = (cg_ref[u] + nt(scaled, low)).astype(BF16)
        now = jnp.exp(cum_ref[u, Q - 1 : Q, :]) * now + piece_ref[u]
    state[...] = now


def join_kernel(me_ref, *refs):
    grad_ref, b_ref = refs[-2:]
    parts = refs[:-2]
    count = len(parts)
    width = grad_ref.shape[1] // count
    total = jnp.zeros(b_ref.shape, F32)
    for d, part in enumerate(parts):
        source = lax.rem(me_ref[0] + count - d, count)
        grad_ref[:, pl.ds(pl.multiple_of(source * width, width), width)] = part[:, :width]
        total = total + part[:, width:].astype(F32)
    b_ref[...] = total


def sum_kernel(in_ref, out_ref):
    total = in_ref[0].astype(F32)
    for j in range(1, in_ref.shape[0]):
        total = total + in_ref[j].astype(F32)
    out_ref[...] = total


def passed_along(value, axis, steps):
    count = lax.axis_size(axis)
    first, last = (max(0, -steps), min(count, count - steps))
    return lax.ppermute(value, axis, [(source, source + steps) for source in range(first, last)])


def body(
    channels,
    input_state_factors,
    c_coeffs,
    step_size_logits,
    a_log,
    skip_gain,
    mix_gain,
    offsets,
    cotangent,
):
    groups = lax.axis_size("head")
    shards = lax.axis_size("ctx")
    tok_dev = channels.shape[0]
    ctx_tok = tok_dev * groups
    spans = ctx_tok // Q
    reach = spans // 2
    heads = a_log.shape[0]
    width = heads * P_SIZE
    in_scale = 1.0 / math.sqrt(N * ctx_tok * shards)

    each = 3
    reach_rows = reach * Q

    def z_swap(value):
        return lax.all_to_all(value, "head", split_axis=0, concat_axis=0, tiled=True)

    def ctx_swap(value):
        return lax.all_to_all(value, "ctx", split_axis=0, concat_axis=0, tiled=True)

    offset_rows = jnp.pad(
        offsets[:reach].astype(BF16), ((0, 16 - reach), (0, width - offsets.shape[1]))
    )
    sent = jnp.concatenate([cotangent[:reach_rows], offset_rows], axis=0)
    later = passed_along(sent, "ctx", -1)

    dt = jnp.pad(
        step_size_logits.T.reshape(groups, heads, tok_dev),
        ((0, 0), (0, 16 - heads), (0, 2 * N - tok_dev)),
    )
    packed = pl.pallas_call(
        pack_kernel,
        grid=(2,),
        in_specs=[
            pl.BlockSpec((tok_dev, N), lambda j: (0, 0)),
            pl.BlockSpec((tok_dev, N), lambda j: (0, 0)),
            pl.BlockSpec((groups // 2, 16, 2 * N), lambda j: (j, 0, 0)),
        ],
        out_specs=pl.BlockSpec((groups // 2, tok_dev + 16, 2 * N), lambda j: (j, 0, 0)),
        out_shape=jax.ShapeDtypeStruct((groups, tok_dev + 16, 2 * N), BF16),
        compiler_params=params(),
        cost_estimate=cost(3.0),
    )(input_state_factors, c_coeffs, dt)
    bcd = z_swap(packed)

    me = lax.axis_index("head").astype(jnp.int32)[None]
    me_spec = pl.BlockSpec(memory_space=pltpu.SMEM)

    def z_shifts(parts):
        moved = [parts[0]]
        for d in range(1, groups):
            pairs = [(source, (source + d) % groups) for source in range(groups)]
            moved.append(lax.ppermute(parts[d], "head", pairs))
        return moved

    chan_parts = pl.pallas_call(
        split_kernel,
        in_specs=[me_spec, pl.BlockSpec(channels.shape, lambda: (0, 0))],
        out_specs=[pl.BlockSpec((tok_dev, width), lambda: (0, 0))] * groups,
        out_shape=[jax.ShapeDtypeStruct((tok_dev, width), BF16)] * groups,
        cost_estimate=cost(3.0),
    )(me, channels)
    x_parts = z_shifts(chan_parts)

    gain = jnp.repeat(mix_gain.T, P_SIZE, axis=1)
    distance = jnp.arange(1, reach + 1, dtype=jnp.int32)
    later_offsets = later[reach_rows : reach_rows + reach, : offsets.shape[1]].astype(jnp.int32)
    all_offsets = jnp.concatenate([offsets, later_offsets], axis=0)
    sources = jnp.stack([all_offsets[d : d + spans] for d in range(1, reach + 1)], axis=1)
    hit = (sources == distance[None, :, None]).astype(F32)
    back_coef = jnp.sum(hit[..., None] * gain[None, None], axis=2)
    back_coef = jnp.pad(back_coef, ((0, 0), (0, 8 - reach), (0, 0)))

    g_rows = mix(
        functools.partial(mix_back_kernel, ((0, spans), (0, reach))),
        (back_coef,),
        [pl.BlockSpec((2, 8, width), lambda i: (i, 0, 0))],
        (cotangent.reshape(spans, Q, width), later[:reach_rows].reshape(reach, Q, width)),
        ((0, spans), (0, reach)),
        2,
        0,
        spans,
        spans,
    )

    dt_rows = jnp.transpose(bcd[:, tok_dev : tok_dev + heads, :tok_dev], (1, 0, 2))
    dt_rows = dt_rows.reshape(heads, ctx_tok)
    log_decay = -jnp.exp(a_log)[:, None] * jax.nn.softplus(dt_rows.astype(F32))

    steps = spans // each

    def coeff_spec(column, order):
        return pl.BlockSpec((2, tok_dev + 16, N), lambda i: (order(i), 0, column))

    def lane_spec(order):
        return pl.BlockSpec((heads, each * Q), lambda i: (0, order(i)))

    def row_spec(columns, order):
        return pl.BlockSpec((each, Q, columns), lambda i: (order(i), 0, 0))

    def whole(shape):
        return pl.BlockSpec(shape, lambda i: (0,) * len(shape))

    def forward(i):
        return i

    def backward(i):
        return steps - 1 - i

    states = [pltpu.VMEM((N, width), F32), pltpu.VMEM((1, width), F32)]
    piece_shape = (shards, N // shards, width + width // (N // shards))
    span_shape = jax.ShapeDtypeStruct((spans, N, width), F32)
    grad_full, cum, cum_rows, back_pieces = pl.pallas_call(
        back_state_kernel,
        grid=(steps,),
        in_specs=[lane_spec(backward), row_spec(width, backward), coeff_spec(1, backward)],
        out_specs=[
            row_spec(width, backward),
            row_spec(width, backward),
            lane_spec(backward),
            whole(piece_shape),
        ],
        out_shape=[
            span_shape,
            span_shape,
            jax.ShapeDtypeStruct((heads, ctx_tok), F32),
            jax.ShapeDtypeStruct(piece_shape, F32),
        ],
        scratch_shapes=states,
        compiler_params=params(),
        cost_estimate=cost(8.0),
    )(log_decay, g_rows, bcd)

    def scan(reverse, decays, got):
        return pl.pallas_call(
            functools.partial(scan_kernel, reverse),
            out_shape=jax.ShapeDtypeStruct((shards, N // shards, width), F32),
            cost_estimate=cost(2.0),
        )(decays, got)

    rev_got = ctx_swap(back_pieces)
    rev_states = scan(True, rev_got, rev_got)
    grad_end = ctx_swap(rev_states)

    own_shape = (shards, N // shards, width)
    any_spec = pl.BlockSpec(memory_space=pl.ANY)
    pieces, x_rows, fore_pieces = pl.pallas_call(
        functools.partial(fore_state_kernel, in_scale),
        grid=(steps,),
        in_specs=[me_spec, row_spec(width, forward), coeff_spec(0, forward)]
        + [any_spec] * groups,
        out_specs=[row_spec(width, forward), row_spec(width, forward), whole(own_shape)],
        out_shape=[
            span_shape,
            jax.ShapeDtypeStruct((spans, Q, width), BF16),
            jax.ShapeDtypeStruct(own_shape, F32),
        ],
        scratch_shapes=[
            pltpu.VMEM((groups, tok_dev, width), BF16),
            states[0],
            pltpu.SemaphoreType.DMA((groups,)),
        ],
        compiler_params=params(),
        cost_estimate=cost(6.0),
    )(me, cum, bcd, *x_parts)
    fwd_got = ctx_swap(fore_pieces)
    fwd_states = scan(False, rev_got, fwd_got)
    state_in = ctx_swap(fwd_states)

    skip = jnp.repeat(skip_gain, P_SIZE)[None, :]
    start_spec = whole((shards, N // shards, width))
    y_part, c_part, *grads = pl.pallas_call(
        functools.partial(span_kernel, in_scale),
        grid=(steps,),
        in_specs=[
            me_spec,
            lane_spec(backward),
            row_spec(width, backward),
            row_spec(width, backward),
            row_spec(width, backward),
            coeff_spec(0, backward),
            coeff_spec(1, backward),
            row_spec(width, backward),
            whole((1, width)),
            start_spec,
        ],
        out_specs=[row_spec(width, backward), row_spec(N, backward)] + [any_spec] * groups,
        out_shape=[
            jax.ShapeDtypeStruct((spans, Q, width), F32),
            jax.ShapeDtypeStruct((spans, Q, N), F32),
        ]
        + [jax.ShapeDtypeStruct((tok_dev, width + N), BF16)] * groups,
        scratch_shapes=[
            pltpu.VMEM((groups, tok_dev, width + N), BF16),
            states[0],
            pltpu.SemaphoreType.DMA((groups,)),
        ],
        compiler_params=params(),
        cost_estimate=cost(20.0),
    )(me, cum_rows, cum, x_rows, g_rows, bcd, bcd, grad_full, skip, grad_end)

    back = z_shifts(grads)

    out_rows, c_rows = pl.pallas_call(
        output_kernel,
        grid=(steps,),
        in_specs=[
            row_spec(width, forward),
            row_spec(width, forward),
            coeff_spec(1, forward),
            row_spec(width, forward),
            row_spec(N, forward),
            row_spec(width, forward),
            start_spec,
        ],
        out_specs=[row_spec(width, forward), row_spec(N, forward)],
        out_shape=[
            jax.ShapeDtypeStruct((spans, Q, width), BF16),
            jax.ShapeDtypeStruct((spans, Q, N), BF16),
        ],
        scratch_shapes=states[:1],
        compiler_params=params(),
        cost_estimate=cost(8.0),
    )(cum, g_rows, bcd, y_part, c_part, pieces, state_in)

    before = passed_along(out_rows[spans - reach :], "ctx", 1)
    c_back = z_swap(c_rows.reshape(groups, tok_dev, N))
    gain_specs = [
        pl.BlockSpec(memory_space=pltpu.SMEM),
        pl.BlockSpec(gain.shape, lambda i: (0, 0)),
    ]
    late = mix(
        functools.partial(mix_fore_kernel, ((0, spans),), reach),
        (offsets, gain),
        gain_specs,
        (out_rows,),
        ((0, spans),),
        2,
        reach,
        spans - reach,
        spans,
    )
    mixed = mix(
        functools.partial(mix_fore_kernel, ((0, reach), (0, reach)), 0),
        (offsets, gain),
        gain_specs,
        (before, out_rows),
        ((0, reach), (0, reach)),
        2,
        0,
        reach,
        spans,
        into=late,
    ).reshape(ctx_tok, width)

    grad_channels, grad_b = pl.pallas_call(
        join_kernel,
        in_specs=[me_spec]
        + [pl.BlockSpec((tok_dev, width + N), lambda: (0, 0))] * groups,
        out_specs=[
            pl.BlockSpec((tok_dev, groups * width), lambda: (0, 0)),
            pl.BlockSpec((tok_dev, N), lambda: (0, 0)),
        ],
        out_shape=[
            jax.ShapeDtypeStruct((tok_dev, groups * width), BF16),
            jax.ShapeDtypeStruct((tok_dev, N), F32),
        ],
        cost_estimate=cost(3.0),
    )(me, *back)
    grad_c = pl.pallas_call(
        sum_kernel,
        out_shape=jax.ShapeDtypeStruct((tok_dev, N), F32),
        cost_estimate=cost(1.0),
    )(c_back)
    return (mixed, grad_channels, grad_b, grad_c)


def solution(mesh):
    placed = (
        P(("ctx", "head"), None),
        P(("ctx", "head"), None),
        P(("ctx", "head"), None),
        P(("ctx", "head"), None),
        P("head"),
        P("head"),
        P("head", None),
        P("ctx", None),
        P("ctx", "head"),
    )
    return jax.shard_map(
        body,
        mesh=mesh,
        in_specs=placed,
        out_specs=(
            P("ctx", "head"),
            P(("ctx", "head"), None),
            P(("ctx", "head"), None),
            P(("ctx", "head"), None),
        ),
        check_vma=False,
    )
```

time: 533 us -> 216 us (0.41)
  the two profiles are of different devices: /device:TPU:8 before, /device:TPU:198 now
where the time goes in v1:
time: 216 us; the launch traced here: 214 us
  waiting for transfers between devices  71.1 us (33%)
  starting transfers between devices  67.4 us (31%)
  Pallas kernels  61.7 us (29%)
  local copies, waits for them, and re-layouts  10.7 us (5%)
    ppermute x14, waiting for transfers between devices, z_shifts(): moved.append(lax.ppermute(parts[d], 'head', pairs))  58.6 us
    all_to_all x4, starting transfers between devices, ctx_swap(): return lax.all_to_all(value, 'ctx', split_axis=0, concat_axis=0, tiled=True)  26.1 us
    ppermute x14, starting transfers between devices, z_shifts(): moved.append(lax.ppermute(parts[d], 'head', pairs))  21 us
    pallas_call x3, Pallas kernels, mix(): pl.pallas_call(kernel, grid=(count // steps,), in_specs=list(specs) + [pl...  14.4 us
    all_to_all x2, starting transfers between devices, z_swap(): lax.all_to_all(value, 'head', split_axis=0, concat_axis=0, tiled=True)  13.6 us
    pallas_call x1, Pallas kernels, body(): pl.pallas_call(functools.partial(span_kernel, in_scale), grid=(steps,), i...  12.2 us
    all_to_all x4, waiting for transfers between devices, ctx_swap(): return lax.all_to_all(value, 'ctx', split_axis=0, concat_axis=0, tiled=True)  9.5 us
    pallas_call x1, Pallas kernels, body(): pl.pallas_call(back_state_kernel, grid=(steps,), in_specs=[lane_spec(back...  8.38 us
  transfers between devices with their start and end apart: 22, of which 9 were waited for; matrix products, arithmetic and copies ran while one was open for 3% of the time, Pallas kernels for 24%

profile of v1, /device:TPU:198, one launch (start us, length us, event | category | flops | bytes accessed | tf_op | source)
XLA Modules:
  0.0 214.0 jit_solution(8813893435253492517)
XLA Ops:
  1.8 4.6 %collective-permute-start = (bf16[784,512]{1,0:T(8,128)(2,1)S(1)}, bf16[784,512]{1,0:T(8,128)(2,1)S(1)}, u32[]{:S(2)}, u32[]{:S(2)}) collective-permute-start(bf16[784,512]{1,0:T(8,128)(2,1)S(1)} %fusion.1), channel_id=1, source_target_pairs={{8,0},{16,8},{24,16},{32,24},{40,32},{48,40},{56,48},{64,56},{72,6... | collective-permute-start | bytes 2408456 | tf_op jit(solution)/shard_map/ppermute | solution.py:408
  8.9 6.3 %all-to-all-start = ((bf16[8,208,256]{2,1,0:T(8,128)(2,1)}), bf16[8,208,256]{2,1,0:T(8,128)(2,1)S(1)}, u32[]{:S(2)}, u32[]{:S(2)}) async-start(bf16[8,208,256]{2,1,0:T(8,128)(2,1)} %shard_map.120), calls=%async_computation | async-start | bytes 1703936 | tf_op jit(solution)/shard_map/all_to_all | solution.py:436
  20.0 4.5 %collective-permute-start.3 = (bf16[192,512]{1,0:T(8,128)(2,1)}, bf16[192,512]{1,0:T(8,128)(2,1)S(1)}, u32[]{:S(2)}, u32[]{:S(2)}) collective-permute-start(bf16[192,512]{1,0:T(8,128)(2,1)} %get-tuple-element.38), channel_id=1, source_target_pairs={{0,3},{1,4},{2,5},{3,6},{4,7},{5,0},{6,1},{7,2},{8,11},{9,12},{10,... | collective-permute-start | bytes 589832 | tf_op jit(solution)/shard_map/ppermute | solution.py:473
  24.6 5.1 %collective-permute-start.5 = (bf16[192,512]{1,0:T(8,128)(2,1)}, bf16[192,512]{1,0:T(8,128)(2,1)S(1)}, u32[]{:S(2)}, u32[]{:S(2)}) collective-permute-start(bf16[192,512]{1,0:T(8,128)(2,1)} %get-tuple-element.40), channel_id=1, source_target_pairs={{0,5},{1,6},{2,7},{3,0},{4,1},{5,2},{6,3},{7,4},{8,13},{9,14},{10,... | collective-permute-start | bytes 589832 | tf_op jit(solution)/shard_map/ppermute | solution.py:473
  32.1 6.4 %shard_map.121.g_ref = bf16[12,128,512]{2,1,0:T(8,128)(2,1)} custom-call(f32[12,8,512]{2,1,0:T(8,128)} %pad.14.coef_ref, bf16[12,128,512]{2,1,0:T(8,128)(2,1)} %bitcast.24, bf16[6,128,512]{2,1,0:T(8,128)(2,1)} %bitcast.25), custom_call_target="tpu_custom_call" | custom-call | flops 3000000000 | tf_op jit(solution)/shard_map/pallas_call | solution.py:142
  44.1 8.1 %collective-permute-done.2.refs_2_ = bf16[192,512]{1,0:T(8,128)(2,1)S(1)} collective-permute-done((bf16[192,512]{1,0:T(8,128)(2,1)}, bf16[192,512]{1,0:T(8,128)(2,1)S(1)}, u32[]{:S(2)}, u32[]{:S(2)}) %collective-permute-start.2) | collective-permute-done | bytes 196640 | tf_op jit(solution)/shard_map/ppermute | solution.py:473
  52.2 8.4 %shard_map.122 = (f32[12,128,512]{2,1,0:T(8,128)}, f32[12,128,512]{2,1,0:T(8,128)}, f32[8,1536]{1,0:T(8,128)}, f32[32,4,640]{2,1,0:T(4,128)}) custom-call(f32[8,1536]{1,0:T(8,128)} %fusion.2.ld_ref, bf16[12,128,512]{2,1,0:T(8,128)(2,1)} %shard_map.121.g_ref, bf16[8,208,256]{2,1,0:T(8,128)(2,1)} %copy-done), custom_call_target="tpu_custom_call" | custom-call | flops 4000000000 | tf_op jit(solution)/shard_map/pallas_call | solution.py:533
  60.6 6.8 %all-to-all-start.1 = ((f32[32,4,640]{2,1,0:T(4,128)}), f32[32,4,640]{2,1,0:T(4,128)S(1)}, u32[]{:S(2)}, u32[]{:S(2)}) async-start(f32[32,4,640]{2,1,0:T(4,128)} %get-tuple-element.45), calls=%async_computation.1 | async-start | bytes 655360 | tf_op jit(solution)/shard_map/all_to_all | solution.py:439
  68.8 6.8 %shard_map.124 = (f32[12,128,512]{2,1,0:T(8,128)}, bf16[12,128,512]{2,1,0:T(8,128)(2,1)}, f32[32,4,512]{2,1,0:T(4,128)}) custom-call(s32[1]{0:T(128)} %bitcast.12.me_ref, f32[12,128,512]{2,1,0:T(8,128)} %get-tuple-element.33.cum_ref, bf16[8,208,256]{2,1,0:T(8,128)(2,1)} %copy-done, bf16[192,512]{1,0:T(8,128)(2,1)} %get-tuple-element.35.refs_0_, ...), custom_call_target="tpu_custom_call" | custom-call | flops 3000000000 | tf_op jit(solution)/shard_map/pallas_call | solution.py:567
  75.6 7.6 %all-to-all-start.3 = ((f32[32,4,512]{2,1,0:T(4,128)}), f32[32,4,512]{2,1,0:T(4,128)S(1)}, u32[]{:S(2)}, u32[]{:S(2)}) async-start(f32[32,4,512]{2,1,0:T(4,128)} %get-tuple-element.49), calls=%async_computation.3 | async-start | bytes 524288 | tf_op jit(solution)/shard_map/all_to_all | solution.py:439
  85.1 5.1 %all-to-all-done.3.in_ref = f32[32,4,512]{2,1,0:T(4,128)S(1)} async-done(((f32[32,4,512]{2,1,0:T(4,128)}), f32[32,4,512]{2,1,0:T(4,128)S(1)}, u32[]{:S(2)}, u32[]{:S(2)}) %all-to-all-start.3) | async-done | bytes 262176 | tf_op jit(solution)/shard_map/all_to_all | solution.py:439
  90.2 5.8 %all-to-all-start.2 = ((f32[32,4,512]{2,1,0:T(4,128)}), f32[32,4,512]{2,1,0:T(4,128)S(1)}, u32[]{:S(2)}, u32[]{:S(2)}) async-start(f32[32,4,512]{2,1,0:T(4,128)} %shard_map.125), calls=%async_computation.2 | async-start | bytes 524288 | tf_op jit(solution)/shard_map/all_to_all | solution.py:439
  98.6 4.4 %all-to-all-done.2.end_ref = f32[32,4,512]{2,1,0:T(4,128)S(1)} async-done(((f32[32,4,512]{2,1,0:T(4,128)}), f32[32,4,512]{2,1,0:T(4,128)S(1)}, u32[]{:S(2)}, u32[]{:S(2)}) %all-to-all-start.2) | async-done | bytes 262176 | tf_op jit(solution)/shard_map/all_to_all | solution.py:439
  103.0 5.8 %all-to-all-start.4 = ((f32[32,4,512]{2,1,0:T(4,128)}), f32[32,4,512]{2,1,0:T(4,128)S(1)}, u32[]{:S(2)}, u32[]{:S(2)}) async-start(f32[32,4,512]{2,1,0:T(4,128)} %shard_map.127), calls=%async_computation.4 | async-start | bytes 524288 | tf_op jit(solution)/shard_map/all_to_all | solution.py:439
  108.8 12.2 %shard_map.126 = (f32[12,128,512]{2,1,0:T(8,128)}, f32[12,128,128]{2,1,0:T(8,128)}, bf16[192,640]{1,0:T(8,128)(2,1)}, bf16[192,640]{1,0:T(8,128)(2,1)}, bf16[192...) custom-call(s32[1]{0:T(128)} %bitcast.12.me_ref, ...), custom_call_target="tpu_custom_call" | custom-call | flops 10000000000 | tf_op jit(solution)/shard_map/pallas_call | solution.py:592
  121.8 7.2 %shard_map.128 = (bf16[12,128,512]{2,1,0:T(8,128)(2,1)}, bf16[12,128,128]{2,1,0:T(8,128)(2,1)}) custom-call(f32[12,128,512]{2,1,0:T(8,128)} %get-tuple-element.33.cum_ref, bf16[12,128,512]{2,1,0:T(8,128)(2,1)} %shard_map.121.g_ref, bf16[8,208,256]{2,1,0:T(8,128)(2,1)} %copy-done, f32[12,128,512]{2,1,0:T(8,128)} %get-tuple-element.46.y_ref, ...), custom_call_target="tpu_custom_call" | custom-call | flops 4000000000 | tf_op jit(solution)/shard_map/pallas_call | solution.py:624
  132.4 7.3 %all-to-all-start.5 = ((bf16[8,192,128]{2,1,0:T(8,128)(2,1)}), bf16[8,192,128]{2,1,0:T(8,128)(2,1)S(1)}, u32[]{:S(2)}, u32[]{:S(2)}) async-start(bf16[8,192,128]{2,1,0:T(8,128)(2,1)} %bitcast.26), calls=%async_computation.5 | async-start | bytes 786432 | tf_op jit(solution)/shard_map/all_to_all | solution.py:436
  141.7 4.5 %collective-permute-start.11 = (bf16[192,640]{1,0:T(8,128)(2,1)S(1)}, bf16[192,640]{1,0:T(8,128)(2,1)S(1)}, u32[]{:S(2)}, u32[]{:S(2)}) collective-permute-start(bf16[192,640]{1,0:T(8,128)(2,1)S(1)} %copy-done.16), channel_id=1, source_target_pairs={{0,3},{1,4},{2,5},{3,6},{4,7},{5,0},{6,1},{7,2},{8,11},{9,12},{10,... | collective-permute-start | bytes 737288 | tf_op jit(solution)/shard_map/ppermute | solution.py:473
  146.3 10.1 %collective-permute-done.9.refs_1_ = bf16[192,640]{1,0:T(8,128)(2,1)S(1)} collective-permute-done((bf16[192,640]{1,0:T(8,128)(2,1)}, bf16[192,640]{1,0:T(8,128)(2,1)S(1)}, u32[]{:S(2)}, u32[]{:S(2)}) %collective-permute-start.9) | collective-permute-done | bytes 245792 | tf_op jit(solution)/shard_map/ppermute | solution.py:473
  157.4 12.0 %collective-permute-done.10.refs_2_ = bf16[192,640]{1,0:T(8,128)(2,1)S(1)} collective-permute-done((bf16[192,640]{1,0:T(8,128)(2,1)S(1)}, bf16[192,640]{1,0:T(8,128)(2,1)S(1)}, u32[]{:S(2)}, u32[]{:S(2)}) %collective-permute-start.10) | collective-permute-done | bytes 245792 | tf_op jit(solution)/shard_map/ppermute | solution.py:473
  169.4 24.9 %collective-permute-done.11.refs_3_ = bf16[192,640]{1,0:T(8,128)(2,1)S(1)} collective-permute-done((bf16[192,640]{1,0:T(8,128)(2,1)S(1)}, bf16[192,640]{1,0:T(8,128)(2,1)S(1)}, u32[]{:S(2)}, u32[]{:S(2)}) %collective-permute-start.11) | collective-permute-done | bytes 245792 | tf_op jit(solution)/shard_map/ppermute | solution.py:473
  195.7 4.0 %shard_map.129.refs_2_ = bf16[12,128,512]{2,1,0:T(8,128)(2,1)} custom-call(s32[12,3]{1,0:T(8,128)} %copy.42.offset_ref, f32[3,512]{1,0:T(4,128)} %copy-done.7, bf16[12,128,512]{2,1,0:T(8,128)(2,1)} %get-tuple-element.50.refs_0_.refs_1_), custom_call_target="tpu_custom_call" | custom-call | flops 1500000000 | tf_op jit(solution)/shard_map/pallas_call | solution.py:142
  199.8 3.2 %collective-permute-done.15.refs_7_ = bf16[192,640]{1,0:T(8,128)(2,1)S(1)} collective-permute-done((bf16[192,640]{1,0:T(8,128)(2,1)S(1)}, bf16[192,640]{1,0:T(8,128)(2,1)S(1)}, u32[]{:S(2)}, u32[]{:S(2)}) %collective-permute-start.15) | collective-permute-done | bytes 245792 | tf_op jit(solution)/shard_map/ppermute | solution.py:473
  209.9 4.0 %shard_map.130 = bf16[12,128,512]{2,1,0:T(8,128)(2,1)} custom-call(s32[12,3]{1,0:T(8,128)} %copy.42.offset_ref, f32[3,512]{1,0:T(4,128)} %copy-done.7, bf16[6,128,512]{2,1,0:T(8,128)(2,1)} %copy-done.11, bf16[12,128,512]{2,1,0:T(8,128)(2,1)} %get-tuple-element.50.refs_0_.refs_1_, ...), custom_call_target="tpu_custom_call", output_to_operand_aliasing={{}: (4, {})} | custom-call | flops 1500000000 | tf_op jit(solution)/shard_map/pallas_call | solution.py:142
  (133 shorter events, 37.6 us)
Async XLA Ops:
  1.8 22.8 %collective-permute-start = (bf16[784,512]{1,0:T(8,128)(2,1)S(1)}, bf16[784,512]{1,0:T(8,128)(2,1)S(1)}, u32[]{:S(2)}, u32[]{:S(2)}) collective-permute-start(bf16[784,512]{1,0:T(8,128)(2,1)S(1)} %fusion.1), channel_id=1, source_target_pairs={{8,0},{16,8},{24,16},{32,24},{40,32},{48,40},{56,48},{64,56},{72,6... | collective-permute-start | bytes 2408456 | tf_op jit(solution)/shard_map/ppermute | solution.py:408
  8.9 32.5 %all-to-all-start = ((bf16[8,208,256]{2,1,0:T(8,128)(2,1)}), bf16[8,208,256]{2,1,0:T(8,128)(2,1)S(1)}, u32[]{:S(2)}, u32[]{:S(2)}) async-start(bf16[8,208,256]{2,1,0:T(8,128)(2,1)} %shard_map.120), calls=%async_computation | async-start | bytes 1703936 | tf_op jit(solution)/shard_map/all_to_all | solution.py:436
  17.9 24.4 %collective-permute-start.1 = (bf16[192,512]{1,0:T(8,128)(2,1)}, bf16[192,512]{1,0:T(8,128)(2,1)S(1)}, u32[]{:S(2)}, u32[]{:S(2)}) collective-permute-start(bf16[192,512]{1,0:T(8,128)(2,1)} %get-tuple-element.36), channel_id=1, source_target_pairs={{0,1},{1,2},{2,3},{3,4},{4,5},{5,6},{6,7},{7,0},{8,9},{9,10},{10,1... | collective-permute-start | bytes 589832 | tf_op jit(solution)/shard_map/ppermute | solution.py:473
  18.5 33.7 %collective-permute-start.2 = (bf16[192,512]{1,0:T(8,128)(2,1)}, bf16[192,512]{1,0:T(8,128)(2,1)S(1)}, u32[]{:S(2)}, u32[]{:S(2)}) collective-permute-start(bf16[192,512]{1,0:T(8,128)(2,1)} %get-tuple-element.37), channel_id=1, source_target_pairs={{0,2},{1,3},{2,4},{3,5},{4,6},{5,7},{6,0},{7,1},{8,10},{9,11},{10,... | collective-permute-start | bytes 589832 | tf_op jit(solution)/shard_map/ppermute | solution.py:473
  20.0 47.9 %collective-permute-start.3 = (bf16[192,512]{1,0:T(8,128)(2,1)}, bf16[192,512]{1,0:T(8,128)(2,1)S(1)}, u32[]{:S(2)}, u32[]{:S(2)}) collective-permute-start(bf16[192,512]{1,0:T(8,128)(2,1)} %get-tuple-element.38), channel_id=1, source_target_pairs={{0,3},{1,4},{2,5},{3,6},{4,7},{5,0},{6,1},{7,2},{8,11},{9,12},{10,... | collective-permute-start | bytes 589832 | tf_op jit(solution)/shard_map/ppermute | solution.py:473
  24.4 43.4 %collective-permute-start.4 = (bf16[192,512]{1,0:T(8,128)(2,1)}, bf16[192,512]{1,0:T(8,128)(2,1)S(1)}, u32[]{:S(2)}, u32[]{:S(2)}) collective-permute-start(bf16[192,512]{1,0:T(8,128)(2,1)} %get-tuple-element.39), channel_id=1, source_target_pairs={{0,4},{1,5},{2,6},{3,7},{4,0},{5,1},{6,2},{7,3},{8,12},{9,13},{10,... | collective-permute-start | bytes 589832 | tf_op jit(solution)/shard_map/ppermute | solution.py:473
  24.6 43.2 %collective-permute-start.5 = (bf16[192,512]{1,0:T(8,128)(2,1)}, bf16[192,512]{1,0:T(8,128)(2,1)S(1)}, u32[]{:S(2)}, u32[]{:S(2)}) collective-permute-start(bf16[192,512]{1,0:T(8,128)(2,1)} %get-tuple-element.40), channel_id=1, source_target_pairs={{0,5},{1,6},{2,7},{3,0},{4,1},{5,2},{6,3},{7,4},{8,13},{9,14},{10,... | collective-permute-start | bytes 589832 | tf_op jit(solution)/shard_map/ppermute | solution.py:473
  42.4 25.5 %collective-permute-start.6 = (bf16[192,512]{1,0:T(8,128)(2,1)S(1)}, bf16[192,512]{1,0:T(8,128)(2,1)S(1)}, u32[]{:S(2)}, u32[]{:S(2)}) collective-permute-start(bf16[192,512]{1,0:T(8,128)(2,1)S(1)} %copy-done.27), channel_id=1, source_target_pairs={{0,6},{1,7},{2,0},{3,1},{4,2},{5,3},{6,4},{7,5},{8,14},{9,15},{10,... | collective-permute-start | bytes 589832 | tf_op jit(solution)/shard_map/ppermute | solution.py:473
  52.2 15.7 %collective-permute-start.7 = (bf16[192,512]{1,0:T(8,128)(2,1)S(1)}, bf16[192,512]{1,0:T(8,128)(2,1)S(1)}, u32[]{:S(2)}, u32[]{:S(2)}) collective-permute-start(bf16[192,512]{1,0:T(8,128)(2,1)S(1)} %copy-done.25), channel_id=1, source_target_pairs={{0,7},{1,0},{2,1},{3,2},{4,3},{5,4},{6,5},{7,6},{8,15},{9,8},{10,9... | collective-permute-start | bytes 589832 | tf_op jit(solution)/shard_map/ppermute | solution.py:473
  60.6 14.9 %all-to-all-start.1 = ((f32[32,4,640]{2,1,0:T(4,128)}), f32[32,4,640]{2,1,0:T(4,128)S(1)}, u32[]{:S(2)}, u32[]{:S(2)}) async-start(f32[32,4,640]{2,1,0:T(4,128)} %get-tuple-element.45), calls=%async_computation.1 | async-start | bytes 655360 | tf_op jit(solution)/shard_map/all_to_all | solution.py:439
  75.6 14.6 %all-to-all-start.3 = ((f32[32,4,512]{2,1,0:T(4,128)}), f32[32,4,512]{2,1,0:T(4,128)S(1)}, u32[]{:S(2)}, u32[]{:S(2)}) async-start(f32[32,4,512]{2,1,0:T(4,128)} %get-tuple-element.49), calls=%async_computation.3 | async-start | bytes 524288 | tf_op jit(solution)/shard_map/all_to_all | solution.py:439
  90.2 12.8 %all-to-all-start.2 = ((f32[32,4,512]{2,1,0:T(4,128)}), f32[32,4,512]{2,1,0:T(4,128)S(1)}, u32[]{:S(2)}, u32[]{:S(2)}) async-start(f32[32,4,512]{2,1,0:T(4,128)} %shard_map.125), calls=%async_computation.2 | async-start | bytes 524288 | tf_op jit(solution)/shard_map/all_to_all | solution.py:439
  103.0 18.1 %all-to-all-start.4 = ((f32[32,4,512]{2,1,0:T(4,128)}), f32[32,4,512]{2,1,0:T(4,128)S(1)}, u32[]{:S(2)}, u32[]{:S(2)}) async-start(f32[32,4,512]{2,1,0:T(4,128)} %shard_map.127), calls=%async_computation.4 | async-start | bytes 524288 | tf_op jit(solution)/shard_map/all_to_all | solution.py:439
  129.0 40.4 %copy-start.13 = (bf16[192,640]{1,0:T(8,128)(2,1)S(1)}, bf16[192,640]{1,0:T(8,128)(2,1)}, u32[]{:S(2)}) copy-start(bf16[192,640]{1,0:T(8,128)(2,1)} %get-tuple-element.57) | copy-start | bytes 737284
  129.1 66.0 %copy-start.12 = (bf16[192,640]{1,0:T(8,128)(2,1)S(1)}, bf16[192,640]{1,0:T(8,128)(2,1)}, u32[]{:S(2)}) copy-start(bf16[192,640]{1,0:T(8,128)(2,1)} %get-tuple-element.58) | copy-start | bytes 737284
  130.4 78.6 %collective-permute-start.8 = (bf16[6,128,512]{2,1,0:T(8,128)(2,1)S(1)}, bf16[6,128,512]{2,1,0:T(8,128)(2,1)S(1)}, u32[]{:S(2)}, u32[]{:S(2)}) collective-permute-start(bf16[6,128,512]{2,1,0:T(8,128)(2,1)S(1)} %slice.48), channel_id=1, source_target_pairs={{0,8},{8,16},{16,24},{24,32},{32,40},{40,48},{48,56},{56,64},{64,7... | collective-permute-start | bytes 2359304 | tf_op jit(solution)/shard_map/ppermute | solution.py:408
  132.4 74.1 %all-to-all-start.5 = ((bf16[8,192,128]{2,1,0:T(8,128)(2,1)}), bf16[8,192,128]{2,1,0:T(8,128)(2,1)S(1)}, u32[]{:S(2)}, u32[]{:S(2)}) async-start(bf16[8,192,128]{2,1,0:T(8,128)(2,1)} %bitcast.26), calls=%async_computation.5 | async-start | bytes 786432 | tf_op jit(solution)/shard_map/all_to_all | solution.py:436
  139.7 16.7 %collective-permute-start.9 = (bf16[192,640]{1,0:T(8,128)(2,1)}, bf16[192,640]{1,0:T(8,128)(2,1)S(1)}, u32[]{:S(2)}, u32[]{:S(2)}) collective-permute-start(bf16[192,640]{1,0:T(8,128)(2,1)} %get-tuple-element.52), channel_id=1, source_target_pairs={{0,1},{1,2},{2,3},{3,4},{4,5},{5,6},{6,7},{7,0},{8,9},{9,10},{10,1... | collective-permute-start | bytes 737288 | tf_op jit(solution)/shard_map/ppermute | solution.py:473
  140.3 29.1 %collective-permute-start.10 = (bf16[192,640]{1,0:T(8,128)(2,1)S(1)}, bf16[192,640]{1,0:T(8,128)(2,1)S(1)}, u32[]{:S(2)}, u32[]{:S(2)}) collective-permute-start(bf16[192,640]{1,0:T(8,128)(2,1)S(1)} %copy-done.17), channel_id=1, source_target_pairs={{0,2},{1,3},{2,4},{3,5},{4,6},{5,7},{6,0},{7,1},{8,10},{9,11},{10,... | collective-permute-start | bytes 737288 | tf_op jit(solution)/shard_map/ppermute | solution.py:473
  141.7 52.6 %collective-permute-start.11 = (bf16[192,640]{1,0:T(8,128)(2,1)S(1)}, bf16[192,640]{1,0:T(8,128)(2,1)S(1)}, u32[]{:S(2)}, u32[]{:S(2)}) collective-permute-start(bf16[192,640]{1,0:T(8,128)(2,1)S(1)} %copy-done.16), channel_id=1, source_target_pairs={{0,3},{1,4},{2,5},{3,6},{4,7},{5,0},{6,1},{7,2},{8,11},{9,12},{10,... | collective-permute-start | bytes 737288 | tf_op jit(solution)/shard_map/ppermute | solution.py:473
  146.2 53.5 %collective-permute-start.12 = (bf16[192,640]{1,0:T(8,128)(2,1)S(1)}, bf16[192,640]{1,0:T(8,128)(2,1)}, u32[]{:S(2)}, u32[]{:S(2)}) collective-permute-start(bf16[192,640]{1,0:T(8,128)(2,1)S(1)} %copy-done.15), channel_id=1, source_target_pairs={{0,4},{1,5},{2,6},{3,7},{4,0},{5,1},{6,2},{7,3},{8,12},{9,13},{10,... | collective-permute-start | bytes 737288 | tf_op jit(solution)/shard_map/ppermute | solution.py:473
  156.4 43.3 %collective-permute-start.13 = (bf16[192,640]{1,0:T(8,128)(2,1)S(1)}, bf16[192,640]{1,0:T(8,128)(2,1)}, u32[]{:S(2)}, u32[]{:S(2)}) collective-permute-start(bf16[192,640]{1,0:T(8,128)(2,1)S(1)} %copy-done.14), channel_id=1, source_target_pairs={{0,5},{1,6},{2,7},{3,0},{4,1},{5,2},{6,3},{7,4},{8,13},{9,14},{10,... | collective-permute-start | bytes 737288 | tf_op jit(solution)/shard_map/ppermute | solution.py:473
  169.4 30.3 %collective-permute-start.14 = (bf16[192,640]{1,0:T(8,128)(2,1)S(1)}, bf16[192,640]{1,0:T(8,128)(2,1)S(1)}, u32[]{:S(2)}, u32[]{:S(2)}) collective-permute-start(bf16[192,640]{1,0:T(8,128)(2,1)S(1)} %copy-done.13), channel_id=1, source_target_pairs={{0,6},{1,7},{2,0},{3,1},{4,2},{5,3},{6,4},{7,5},{8,14},{9,15},{10,... | collective-permute-start | bytes 737288 | tf_op jit(solution)/shard_map/ppermute | solution.py:473
  195.0 7.9 %collective-permute-start.15 = (bf16[192,640]{1,0:T(8,128)(2,1)S(1)}, bf16[192,640]{1,0:T(8,128)(2,1)S(1)}, u32[]{:S(2)}, u32[]{:S(2)}) collective-permute-start(bf16[192,640]{1,0:T(8,128)(2,1)S(1)} %copy-done.12), channel_id=1, source_target_pairs={{0,7},{1,0},{2,1},{3,2},{4,3},{5,4},{6,5},{7,6},{8,15},{9,8},{10,9... | collective-permute-start | bytes 737288 | tf_op jit(solution)/shard_map/ppermute | solution.py:473
  (32 other events, 297.2 us)

commit v2 on v1

--- a/solution.py
+++ b/solution.py
@@ -21,8 +21,11 @@
     return pl.CostEstimate(flops=int(us * 5.0e8), bytes_accessed=int(moved), transcendentals=0)
 
 
-def params(**kw):
-    return pltpu.CompilerParams(dimension_semantics=("arbitrary",), **kw)
+def params(grid=True, small=False):
+    semantics = ("arbitrary",) if grid else None
+    if small:
+        return pltpu.CompilerParams(dimension_semantics=semantics, vmem_limit_bytes=12 << 20)
+    return pltpu.CompilerParams(dimension_semantics=semantics)
 
 
 def nn(a, b):
@@ -102,6 +105,10 @@
         copy.wait()
 
 
+def block_rows(ref, block):
+    return ref[pl.ds(pl.multiple_of(block * Q, Q), Q), :]
+
+
 def mix_back_kernel(places, coef_ref, *refs):
     out_ref, ext, sems = refs[-3], refs[-2], refs[-1]
     i = pl.program_id(0)
@@ -112,9 +119,10 @@
         gather_copies(refs[:-3], places, ext, sems)
 
     for u in range(steps):
-        acc = ext[steps * i + u].astype(F32)
+        block = steps * i + u
+        acc = block_rows(ext, block).astype(F32)
         for d in range(1, 7):
-            acc = acc + coef_ref[u, d - 1 : d, :] * ext[steps * i + u + d].astype(F32)
+            acc = acc + coef_ref[u, d - 1 : d, :] * block_rows(ext, block + d).astype(F32)
         out_ref[u] = acc.astype(BF16)
 
 
@@ -129,9 +137,9 @@
 
     for u in range(steps):
         block = steps * i + u
-        acc = ext[6 + block].astype(F32)
+        acc = block_rows(ext, 6 + block).astype(F32)
         for k in range(offset_ref.shape[1]):
-            picked = ext[6 + block - offset_ref[first + block, k]]
+            picked = block_rows(ext, 6 + block - offset_ref[first + block, k])
             acc = acc + gain_ref[k : k + 1, :] * picked.astype(F32)
         out_ref[u] = acc.astype(BF16)
 
@@ -146,11 +154,11 @@
         out_specs=pl.BlockSpec((steps, Q, width), lambda i: (i + first // steps, 0, 0)),
         out_shape=jax.ShapeDtypeStruct((total, Q, width), BF16),
         scratch_shapes=[
-            pltpu.VMEM((sum(length for _, length in places), Q, width), BF16),
+            pltpu.VMEM((sum(length for _, length in places), width), BF16),
             pltpu.SemaphoreType.DMA((len(places),)),
         ],
         input_output_aliases={} if into is None else {len(args) - 1: 0},
-        compiler_params=params(),
+        compiler_params=params(True, True),
         cost_estimate=cost(0.5 * count),
     )(*args)
 
@@ -183,7 +191,7 @@
     return jnp.concatenate([ref[0, :used], ref[1, :used]], axis=0)
 
 
-def back_state_kernel(ld_ref, g_ref, c_ref, full_ref, cum_ref, row_ref, out_ref, state, total):
+def back_state_kernel(ld_ref, g_ref, c_ref, full_ref, col_ref, row_ref, out_ref, state, total):
     heads = ld_ref.shape[0]
     i = pl.program_id(0)
 
@@ -199,11 +207,11 @@
         part = slice(u * Q, (u + 1) * Q)
         rows, cols = cumulative(ld_ref[:, part])
         row_ref[:, part] = rows
+        col_ref[u, :, :heads] = cols
         cum = spread_heads(cols, heads)
-        cum_ref[u] = cum
         scaled = (g_ref[u].astype(F32) * jnp.exp(cum)).astype(BF16)
         full = tn(all_c[part], scaled)
-        full_ref[u] = full
+        full_ref[u] = full.astype(BF16)
         fulls.append(full)
         lasts.append(cum[Q - 1 : Q, :])
     now = state[...]
@@ -217,7 +225,7 @@
         put_pieces(out_ref, state[...], fold_row(jnp.exp(total[...]), out_ref.shape[1]))
 
 
-def fore_state_kernel(in_scale, me_ref, cum_ref, b_ref, *refs):
+def fore_state_kernel(in_scale, heads, me_ref, col_ref, b_ref, *refs):
     piece_ref, x_ref, out_ref, x_all, state, sems = refs[-6:]
     parts = refs[:-6]
     count = len(parts)
@@ -241,12 +249,13 @@
     lasts = []
     for u in range(x_ref.shape[0]):
         part = slice(u * Q, (u + 1) * Q)
-        last = cum_ref[u, Q - 1 : Q, :]
+        cum = spread_heads(col_ref[u], heads)
+        last = cum[Q - 1 : Q, :]
         x = all_x[part]
         x_ref[u] = x
-        scaled = (x.astype(F32) * jnp.exp(last - cum_ref[u])).astype(BF16)
+        scaled = (x.astype(F32) * jnp.exp(last - cum)).astype(BF16)
         piece = tn(all_b[part], scaled) * in_scale
-        piece_ref[u] = piece
+        piece_ref[u] = piece.astype(BF16)
         pieces.append(piece)
         lasts.append(last)
     now = state[...]
@@ -273,7 +282,7 @@
     in_scale,
     me_ref,
     row_ref,
-    cum_ref,
+    col_ref,
     x_ref,
     g_ref,
     b_ref,
@@ -319,15 +328,19 @@
         after_low = after.astype(BF16)
         inter = nn(b, after_low) * in_scale
         grad_scores = jnp.zeros((Q, Q), F32)
+        cols = col_ref[u]
         x_ends = []
+        factors = []
         for pair in range(heads // 2):
             lanes = slice(pair * 2 * P_SIZE, (pair + 1) * 2 * P_SIZE)
             x = x_ref[u, :, lanes]
             g = g_ref[u, :, lanes]
             zero = jnp.zeros_like(x)
-            cum = cum_ref[u, :, lanes]
-            gap0 = lane_fill(cum, 0) - row_ref[2 * pair : 2 * pair + 1, part]
-            gap1 = lane_fill(cum, P_SIZE) - row_ref[2 * pair + 1 : 2 * pair + 2, part]
+            first = lane_fill(cols, 2 * pair)
+            second = lane_fill(cols, 2 * pair + 1)
+            cum = jnp.where(mask, first, second)
+            gap0 = first - row_ref[2 * pair : 2 * pair + 1, part]
+            gap1 = second - row_ref[2 * pair + 1 : 2 * pair + 2, part]
             decay0 = jnp.exp(jnp.where(causal, gap0, -1e30))
             decay1 = jnp.exp(jnp.where(causal, gap1, -1e30))
             weight0 = (scores * decay0).astype(BF16)
@@ -336,13 +349,14 @@
             g_two = jnp.concatenate([jnp.where(mask, g, zero), jnp.where(mask, zero, g)], axis=0)
             skip = skip_ref[0:1, lanes]
             xf = x.astype(F32)
-            y_ref[u, :, lanes] = (
-                nn(jnp.concatenate([weight0, weight1], axis=1), x_two) + skip * xf
-            )
+            y = nn(jnp.concatenate([weight0, weight1], axis=1), x_two) + skip * xf
+            y_ref[u, :, lanes] = y.astype(BF16)
             d_weights = nt(g_two, x)
             grad_scores = grad_scores + d_weights[:Q] * decay0 + d_weights[Q:] * decay1
             local = tn(jnp.concatenate([weight0, weight1], axis=0), g_two)
-            end_decay = jnp.exp(cum[Q - 1 : Q, :] - cum)
+            last = cum[Q - 1 : Q, :]
+            end_decay = jnp.exp(last - cum)
+            factors.append(jnp.exp(last))
             grad = local + end_decay * inter[:, lanes] + skip * g.astype(F32)
             put_grad(u, lanes, grad.astype(BF16))
             x_ends.append((xf * end_decay).astype(BF16))
@@ -350,36 +364,69 @@
         b_sum = nt(jnp.concatenate(x_ends, axis=1), after_low) * in_scale
         put_grad(u, slice(heads * P_SIZE, None), (b_sum + tn(narrow, c)).astype(BF16))
         cg_ref[u] = nn(narrow, b)
-        state[...] = jnp.exp(cum_ref[u, Q - 1 : Q, :]) * after + full_ref[u]
+        state[...] = jnp.concatenate(factors, axis=1) * after + full_ref[u].astype(F32)
+
+    for d, ref in enumerate(grad_refs):
+
+        @pl.when(jnp.logical_or(slots[0] == d, slots[1] == d))
+        def _(d=d, ref=ref):
+            pltpu.make_async_copy(grads.at[d], ref, sems.at[d]).start()
 
     @pl.when(i == pl.num_programs(0) - 1)
     def _():
-        copies = [
-            pltpu.make_async_copy(grads.at[d], ref, sems.at[d]) for d, ref in enumerate(grad_refs)
-        ]
-        for copy in copies:
-            copy.start()
-        for copy in copies:
-            copy.wait()
+        for d, ref in enumerate(grad_refs):
+            pltpu.make_async_copy(grads.at[d], ref, sems.at[d]).wait()
 
 
 def output_kernel(
-    cum_ref, g_ref, c_ref, y_ref, cg_ref, piece_ref, start_ref, out_ref, c_out_ref, state
+    heads,
+    offset_ref,
+    gain_ref,
+    col_ref,
+    g_ref,
+    c_ref,
+    y_ref,
+    cg_ref,
+    piece_ref,
+    start_ref,
+    out_ref,
+    tail_ref,
+    mixed_ref,
+    c_out_ref,
+    state,
+    kept,
 ):
-    @pl.when(pl.program_id(0) == 0)
+    i = pl.program_id(0)
+    steps = g_ref.shape[0]
+
+    @pl.when(i == 0)
     def _():
         state[...] = take_pieces(start_ref)
 
     all_c = token_rows(c_ref)
     now = state[...]
-    for u in range(g_ref.shape[0]):
-        from_start = jnp.exp(cum_ref[u])
+    for u in range(steps):
+        cum = spread_heads(col_ref[u], heads)
+        from_start = jnp.exp(cum)
         low = now.astype(BF16)
-        out_ref[u] = (y_ref[u] + nn(all_c[u * Q : (u + 1) * Q], low) * from_start).astype(BF16)
+        out = (y_ref[u].astype(F32) + nn(all_c[u * Q : (u + 1) * Q], low) * from_start).astype(BF16)
+        out_ref[u] = out
+        tail_ref[u] = out
+        kept[steps * i + u] = out
         scaled = (g_ref[u].astype(F32) * from_start).astype(BF16)
         c_out_ref[u] = (cg_ref[u] + nt(scaled, low)).astype(BF16)
-        now = jnp.exp(cum_ref[u, Q - 1 : Q, :]) * now + piece_ref[u]
+        now = jnp.exp(cum[Q - 1 : Q, :]) * now + piece_ref[u].astype(F32)
     state[...] = now
+
+    @pl.when(steps * i >= 6)
+    def _():
+        for u in range(steps):
+            block = steps * i + u
+            acc = kept[block].astype(F32)
+            for k in range(offset_ref.shape[1]):
+                picked = kept[block - offset_ref[block, k]]
+                acc = acc + gain_ref[k : k + 1, :] * picked.astype(F32)
+            mixed_ref[u] = acc.astype(BF16)
 
 
 def join_kernel(me_ref, *refs):
@@ -458,7 +505,7 @@
         ],
         out_specs=pl.BlockSpec((groups // 2, tok_dev + 16, 2 * N), lambda j: (j, 0, 0)),
         out_shape=jax.ShapeDtypeStruct((groups, tok_dev + 16, 2 * N), BF16),
-        compiler_params=params(),
+        compiler_params=params(True, True),
         cost_estimate=cost(3.0),
     )(input_state_factors, c_coeffs, dt)
     bcd = z_swap(packed)
@@ -478,6 +525,7 @@
         in_specs=[me_spec, pl.BlockSpec(channels.shape, lambda: (0, 0))],
         out_specs=[pl.BlockSpec((tok_dev, width), lambda: (0, 0))] * groups,
         out_shape=[jax.ShapeDtypeStruct((tok_dev, width), BF16)] * groups,
+        compiler_params=params(False),
         cost_estimate=cost(3.0),
     )(me, channels)
     x_parts = z_shifts(chan_parts)
@@ -492,11 +540,11 @@
     back_coef = jnp.pad(back_coef, ((0, 0), (0, 8 - reach), (0, 0)))
 
     g_rows = mix(
-        functools.partial(mix_back_kernel, ((0, spans), (0, reach))),
+        functools.partial(mix_back_kernel, ((0, ctx_tok), (0, reach_rows))),
         (back_coef,),
         [pl.BlockSpec((2, 8, width), lambda i: (i, 0, 0))],
-        (cotangent.reshape(spans, Q, width), later[:reach_rows].reshape(reach, Q, width)),
-        ((0, spans), (0, reach)),
+        (cotangent, later),
+        ((0, ctx_tok), (0, reach_rows)),
         2,
         0,
         spans,
@@ -529,20 +577,20 @@
 
     states = [pltpu.VMEM((N, width), F32), pltpu.VMEM((1, width), F32)]
     piece_shape = (shards, N // shards, width + width // (N // shards))
-    span_shape = jax.ShapeDtypeStruct((spans, N, width), F32)
-    grad_full, cum, cum_rows, back_pieces = pl.pallas_call(
+    span_shape = jax.ShapeDtypeStruct((spans, N, width), BF16)
+    grad_full, cum_cols, cum_rows, back_pieces = pl.pallas_call(
         back_state_kernel,
         grid=(steps,),
         in_specs=[lane_spec(backward), row_spec(width, backward), coeff_spec(1, backward)],
         out_specs=[
             row_spec(width, backward),
-            row_spec(width, backward),
+            row_spec(N, backward),
             lane_spec(backward),
             whole(piece_shape),
         ],
         out_shape=[
             span_shape,
-            span_shape,
+            jax.ShapeDtypeStruct((spans, Q, N), F32),
             jax.ShapeDtypeStruct((heads, ctx_tok), F32),
             jax.ShapeDtypeStruct(piece_shape, F32),
         ],
@@ -555,6 +603,7 @@
         return pl.pallas_call(
             functools.partial(scan_kernel, reverse),
             out_shape=jax.ShapeDtypeStruct((shards, N // shards, width), F32),
+            compiler_params=params(False, True),
             cost_estimate=cost(2.0),
         )(decays, got)
 
@@ -565,9 +614,9 @@
     own_shape = (shards, N // shards, width)
     any_spec = pl.BlockSpec(memory_space=pl.ANY)
     pieces, x_rows, fore_pieces = pl.pallas_call(
-        functools.partial(fore_state_kernel, in_scale),
+        functools.partial(fore_state_kernel, in_scale, heads),
         grid=(steps,),
-        in_specs=[me_spec, row_spec(width, forward), coeff_spec(0, forward)]
+        in_specs=[me_spec, row_spec(N, forward), coeff_spec(0, forward)]
         + [any_spec] * groups,
         out_specs=[row_spec(width, forward), row_spec(width, forward), whole(own_shape)],
         out_shape=[
@@ -582,7 +631,7 @@
         ],
         compiler_params=params(),
         cost_estimate=cost(6.0),
-    )(me, cum, bcd, *x_parts)
+    )(me, cum_cols, bcd, *x_parts)
     fwd_got = ctx_swap(fore_pieces)
     fwd_states = scan(False, rev_got, fwd_got)
     state_in = ctx_swap(fwd_states)
@@ -595,7 +644,7 @@
         in_specs=[
             me_spec,
             lane_spec(backward),
-            row_spec(width, backward),
+            row_spec(N, backward),
             row_spec(width, backward),
             row_spec(width, backward),
             coeff_spec(0, backward),
@@ -606,7 +655,7 @@
         ],
         out_specs=[row_spec(width, backward), row_spec(N, backward)] + [any_spec] * groups,
         out_shape=[
-            jax.ShapeDtypeStruct((spans, Q, width), F32),
+            jax.ShapeDtypeStruct((spans, Q, width), BF16),
             jax.ShapeDtypeStruct((spans, Q, N), F32),
         ]
         + [jax.ShapeDtypeStruct((tok_dev, width + N), BF16)] * groups,
@@ -617,15 +666,21 @@
         ],
         compiler_params=params(),
         cost_estimate=cost(20.0),
-    )(me, cum_rows, cum, x_rows, g_rows, bcd, bcd, grad_full, skip, grad_end)
+    )(me, cum_rows, cum_cols, x_rows, g_rows, bcd, bcd, grad_full, skip, grad_end)
 
     back = z_shifts(grads)
 
-    out_rows, c_rows = pl.pallas_call(
-        output_kernel,
+    gain_specs = [
+        pl.BlockSpec(memory_space=pltpu.SMEM),
+        pl.BlockSpec(gain.shape, lambda i: (0, 0)),
+    ]
+    skipped = steps // 2
+    out_rows, out_tail, late, c_rows = pl.pallas_call(
+        functools.partial(output_kernel, heads),
         grid=(steps,),
-        in_specs=[
-            row_spec(width, forward),
+        in_specs=gain_specs
+        + [
+            row_spec(N, forward),
             row_spec(width, forward),
             coeff_spec(1, forward),
             row_spec(width, forward),
@@ -633,39 +688,31 @@
             row_spec(width, forward),
             start_spec,
         ],
-        out_specs=[row_spec(width, forward), row_spec(N, forward)],
+        out_specs=[
+            row_spec(width, forward),
+            row_spec(width, lambda i: jnp.maximum(i - skipped, 0)),
+            row_spec(width, lambda i: jnp.maximum(i, skipped)),
+            row_spec(N, forward),
+        ],
         out_shape=[
             jax.ShapeDtypeStruct((spans, Q, width), BF16),
+            jax.ShapeDtypeStruct((reach, Q, width), BF16),
+            jax.ShapeDtypeStruct((spans, Q, width), BF16),
             jax.ShapeDtypeStruct((spans, Q, N), BF16),
         ],
-        scratch_shapes=states[:1],
+        scratch_shapes=[states[0], pltpu.VMEM((spans, Q, width), BF16)],
         compiler_params=params(),
         cost_estimate=cost(8.0),
-    )(cum, g_rows, bcd, y_part, c_part, pieces, state_in)
-
-    before = passed_along(out_rows[spans - reach :], "ctx", 1)
+    )(offsets, gain, cum_cols, g_rows, bcd, y_part, c_part, pieces, state_in)
+
+    before = passed_along(out_tail, "ctx", 1)
     c_back = z_swap(c_rows.reshape(groups, tok_dev, N))
-    gain_specs = [
-        pl.BlockSpec(memory_space=pltpu.SMEM),
-        pl.BlockSpec(gain.shape, lambda i: (0, 0)),
-    ]
-    late = mix(
-        functools.partial(mix_fore_kernel, ((0, spans),), reach),
+    mixed = mix(
+        functools.partial(mix_fore_kernel, ((0, reach_rows), (0, reach_rows)), 0),
         (offsets, gain),
         gain_specs,
-        (out_rows,),
-        ((0, spans),),
-        2,
-        reach,
-        spans - reach,
-        spans,
-    )
-    mixed = mix(
-        functools.partial(mix_fore_kernel, ((0, reach), (0, reach)), 0),
-        (offsets, gain),
-        gain_specs,
-        (before, out_rows),
-        ((0, reach), (0, reach)),
+        (before.reshape(reach_rows, width), out_rows.reshape(ctx_tok, width)),
+        ((0, reach_rows), (0, reach_rows)),
         2,
         0,
         reach,
@@ -685,11 +732,13 @@
             jax.ShapeDtypeStruct((tok_dev, groups * width), BF16),
             jax.ShapeDtypeStruct((tok_dev, N), F32),
         ],
+        compiler_params=params(False),
         cost_estimate=cost(3.0),
     )(me, *back)
     grad_c = pl.pallas_call(
         sum_kernel,
         out_shape=jax.ShapeDtypeStruct((tok_dev, N), F32),
+        compiler_params=params(False, True),
         cost_estimate=cost(1.0),
     )(c_back)
     return (mixed, grad_channels, grad_b, grad_c)

time: 216 us -> 208 us (0.963)
  the two profiles are of different devices: /device:TPU:198 before, /device:TPU:8 now
where the time goes in v2:
time: 208 us; the launch traced here: 207 us
  starting transfers between devices  86.8 us (42%)
  waiting for transfers between devices  62 us (30%)
  Pallas kernels  47.6 us (23%)
  local copies, waits for them, and re-layouts  7.23 us (3%)
    ppermute x14, starting transfers between devices, z_shifts(): moved.append(lax.ppermute(parts[d], 'head', pairs))  44.9 us
    ppermute x14, waiting for transfers between devices, z_shifts(): moved.append(lax.ppermute(parts[d], 'head', pairs))  44.1 us
    all_to_all x4, starting transfers between devices, ctx_swap(): return lax.all_to_all(value, 'ctx', split_axis=0, concat_axis=0, tiled=True)  26 us
    all_to_all x2, starting transfers between devices, z_swap(): lax.all_to_all(value, 'head', split_axis=0, concat_axis=0, tiled=True)  11.9 us
    all_to_all x4, waiting for transfers between devices, ctx_swap(): return lax.all_to_all(value, 'ctx', split_axis=0, concat_axis=0, tiled=True)  11.9 us
    pallas_call x1, Pallas kernels, body(): pl.pallas_call(functools.partial(span_kernel, in_scale), grid=(steps,), i...  11.3 us
    pallas_call x1, Pallas kernels, body(): pl.pallas_call(back_state_kernel, grid=(steps,), in_specs=[lane_spec(back...  7.97 us
    pallas_call x1, Pallas kernels, body(): pl.pallas_call(functools.partial(output_kernel, heads), grid=(steps,), in...  7.44 us
  transfers between devices with their start and end apart: 22, of which 12 were waited for; matrix products, arithmetic and copies ran while one was open for 1% of the time, Pallas kernels for 18%

profile of v2, /device:TPU:8, one launch (start us, length us, event | category | flops | bytes accessed | tf_op | source)
XLA Modules:
  0.0 206.9 jit_solution(8481961514687858484)
XLA Ops:
  5.7 8.5 %all-to-all-start = ((bf16[8,208,256]{2,1,0:T(8,128)(2,1)}), bf16[8,208,256]{2,1,0:T(8,128)(2,1)S(1)}, u32[]{:S(2)}, u32[]{:S(2)}) async-start(bf16[8,208,256]{2,1,0:T(8,128)(2,1)} %shard_map.120), calls=%async_computation | async-start | bytes 1703936 | tf_op jit(solution)/shard_map/all_to_all | solution.py:483
  33.5 6.0 %all-to-all-done.c_ref.b_ref = bf16[8,208,256]{2,1,0:T(8,128)(2,1)S(1)} async-done(((bf16[8,208,256]{2,1,0:T(8,128)(2,1)}), bf16[8,208,256]{2,1,0:T(8,128)(2,1)S(1)}, u32[]{:S(2)}, u32[]{:S(2)}) %all-to-all-start) | async-done | bytes 852000 | tf_op jit(solution)/shard_map/all_to_all | solution.py:483
  42.0 8.6 %collective-permute-start.6 = (bf16[192,512]{1,0:T(8,128)(2,1)}, bf16[192,512]{1,0:T(8,128)(2,1)S(1)}, u32[]{:S(2)}, u32[]{:S(2)}) collective-permute-start(bf16[192,512]{1,0:T(8,128)(2,1)} %get-tuple-element.43), channel_id=1, source_target_pairs={{0,6},{1,7},{2,0},{3,1},{4,2},{5,3},{6,4},{7,5},{8,14},{9,15},{10,... | collective-permute-start | bytes 589832 | tf_op jit(solution)/shard_map/ppermute | solution.py:520
  52.7 8.0 %shard_map.122 = (bf16[12,128,512]{2,1,0:T(8,128)(2,1)}, f32[12,128,128]{2,1,0:T(8,128)}, f32[8,1536]{1,0:T(8,128)}, f32[32,4,640]{2,1,0:T(4,128)}) custom-call(f32[8,1536]{1,0:T(8,128)} %fusion.2.ld_ref, bf16[12,128,512]{2,1,0:T(8,128)(2,1)} %copy-done.7, bf16[8,208,256]{2,1,0:T(8,128)(2,1)} %copy-done.8), custom_call_target="tpu_custom_call" | custom-call | flops 4000000000 | tf_op jit(solution)/shard_map/pallas_call | solution.py:581
  60.7 7.8 %all-to-all-start.1 = ((f32[32,4,640]{2,1,0:T(4,128)}), f32[32,4,640]{2,1,0:T(4,128)S(1)}, u32[]{:S(2)}, u32[]{:S(2)}) async-start(f32[32,4,640]{2,1,0:T(4,128)} %get-tuple-element.47), calls=%async_computation.1 | async-start | bytes 655360 | tf_op jit(solution)/shard_map/all_to_all | solution.py:486
  68.5 4.7 %collective-permute-done.4.refs_4_ = bf16[192,512]{1,0:T(8,128)(2,1)} collective-permute-done((bf16[192,512]{1,0:T(8,128)(2,1)}, bf16[192,512]{1,0:T(8,128)(2,1)}, u32[]{:S(2)}, u32[]{:S(2)}) %collective-permute-start.4) | collective-permute-done | bytes 196640 | tf_op jit(solution)/shard_map/ppermute | solution.py:520
  74.0 7.2 %shard_map.124 = (bf16[12,128,512]{2,1,0:T(8,128)(2,1)}, bf16[12,128,512]{2,1,0:T(8,128)(2,1)}, f32[32,4,512]{2,1,0:T(4,128)}) custom-call(s32[1]{0:T(128)} %bitcast.10.me_ref, f32[12,128,128]{2,1,0:T(8,128)} %get-tuple-element.35.col_ref, bf16[8,208,256]{2,1,0:T(8,128)(2,1)} %copy-done.8, bf16[192,512]{1,0:T(8,128)(2,1)} %get-tuple-element.37.refs_0_, ...), custom_call_target="tpu_custom_call" | custom-call | flops 3000000000 | tf_op jit(solution)/shard_map/pallas_call | solution.py:616
  81.2 7.5 %all-to-all-start.3 = ((f32[32,4,512]{2,1,0:T(4,128)}), f32[32,4,512]{2,1,0:T(4,128)S(1)}, u32[]{:S(2)}, u32[]{:S(2)}) async-start(f32[32,4,512]{2,1,0:T(4,128)} %get-tuple-element.51), calls=%async_computation.3 | async-start | bytes 524288 | tf_op jit(solution)/shard_map/all_to_all | solution.py:486
  89.5 6.6 %all-to-all-done.3.in_ref = f32[32,4,512]{2,1,0:T(4,128)S(1)} async-done(((f32[32,4,512]{2,1,0:T(4,128)}), f32[32,4,512]{2,1,0:T(4,128)S(1)}, u32[]{:S(2)}, u32[]{:S(2)}) %all-to-all-start.3) | async-done | bytes 262176 | tf_op jit(solution)/shard_map/all_to_all | solution.py:486
  96.1 5.3 %all-to-all-start.2 = ((f32[32,4,512]{2,1,0:T(4,128)}), f32[32,4,512]{2,1,0:T(4,128)S(1)}, u32[]{:S(2)}, u32[]{:S(2)}) async-start(f32[32,4,512]{2,1,0:T(4,128)} %shard_map.125), calls=%async_computation.2 | async-start | bytes 524288 | tf_op jit(solution)/shard_map/all_to_all | solution.py:486
  103.6 5.3 %all-to-all-done.2.end_ref = f32[32,4,512]{2,1,0:T(4,128)S(1)} async-done(((f32[32,4,512]{2,1,0:T(4,128)}), f32[32,4,512]{2,1,0:T(4,128)S(1)}, u32[]{:S(2)}, u32[]{:S(2)}) %all-to-all-start.2) | async-done | bytes 262176 | tf_op jit(solution)/shard_map/all_to_all | solution.py:486
  108.9 5.3 %all-to-all-start.4 = ((f32[32,4,512]{2,1,0:T(4,128)}), f32[32,4,512]{2,1,0:T(4,128)S(1)}, u32[]{:S(2)}, u32[]{:S(2)}) async-start(f32[32,4,512]{2,1,0:T(4,128)} %shard_map.127), calls=%async_computation.4 | async-start | bytes 524288 | tf_op jit(solution)/shard_map/all_to_all | solution.py:486
  114.2 11.3 %shard_map.126 = (bf16[12,128,512]{2,1,0:T(8,128)(2,1)}, f32[12,128,128]{2,1,0:T(8,128)}, bf16[192,640]{1,0:T(8,128)(2,1)}, bf16[192,640]{1,0:T(8,128)(2,1)}, bf...) custom-call(s32[1]{0:T(128)} %bitcast.10.me_ref, ...), custom_call_target="tpu_custom_call" | custom-call | flops 10000000000 | tf_op jit(solution)/shard_map/pallas_call | solution.py:641
  126.2 7.4 %shard_map.128 = (bf16[12,128,512]{2,1,0:T(8,128)(2,1)}, bf16[6,128,512]{2,1,0:T(8,128)(2,1)}, bf16[12,128,512]{2,1,0:T(8,128)(2,1)}, bf16[12,128,128]{2,1,0:T(8,128)(2,1)}) custom-call(s32[12,3]{1,0:T(8,128)} %copy.42.offset_ref, f32[3,512]{1,0:T(4,128)} %copy-done.1, f32[12,128,128]{2,1,0:T(8,128)} %get-tuple-element.35.col_ref, ...), custom_call_target="tpu_custom_call" | custom-call | flops 4000000000 | tf_op jit(solution)/shard_map/pallas_call | solution.py:678
  135.7 3.5 %all-to-all-start.5 = ((bf16[8,192,128]{2,1,0:T(8,128)(2,1)}), bf16[8,192,128]{2,1,0:T(8,128)(2,1)S(1)}, u32[]{:S(2)}, u32[]{:S(2)}) async-start(bf16[8,192,128]{2,1,0:T(8,128)(2,1)} %bitcast.26), calls=%async_computation.5 | async-start | bytes 786432 | tf_op jit(solution)/shard_map/all_to_all | solution.py:483
  142.0 3.6 %collective-permute-start.11 = (bf16[192,640]{1,0:T(8,128)(2,1)S(1)}, bf16[192,640]{1,0:T(8,128)(2,1)S(1)}, u32[]{:S(2)}, u32[]{:S(2)}) collective-permute-start(bf16[192,640]{1,0:T(8,128)(2,1)S(1)} %copy-done.20), channel_id=1, source_target_pairs={{0,3},{1,4},{2,5},{3,6},{4,7},{5,0},{6,1},{7,2},{8,11},{9,12},{10,... | collective-permute-start | bytes 737288 | tf_op jit(solution)/shard_map/ppermute | solution.py:520
  147.0 3.6 %collective-permute-start.13 = (bf16[192,640]{1,0:T(8,128)(2,1)S(1)}, bf16[192,640]{1,0:T(8,128)(2,1)S(1)}, u32[]{:S(2)}, u32[]{:S(2)}) collective-permute-start(bf16[192,640]{1,0:T(8,128)(2,1)S(1)} %copy-done.18), channel_id=1, source_target_pairs={{0,5},{1,6},{2,7},{3,0},{4,1},{5,2},{6,3},{7,4},{8,13},{9,14},{10,... | collective-permute-start | bytes 737288 | tf_op jit(solution)/shard_map/ppermute | solution.py:520
  150.7 9.8 %collective-permute-done.10.refs_2_ = bf16[192,640]{1,0:T(8,128)(2,1)S(1)} collective-permute-done((bf16[192,640]{1,0:T(8,128)(2,1)S(1)}, bf16[192,640]{1,0:T(8,128)(2,1)S(1)}, u32[]{:S(2)}, u32[]{:S(2)}) %collective-permute-start.10) | collective-permute-done | bytes 245792 | tf_op jit(solution)/shard_map/ppermute | solution.py:520
  160.5 8.3 %collective-permute-start.14 = (bf16[192,640]{1,0:T(8,128)(2,1)S(1)}, bf16[192,640]{1,0:T(8,128)(2,1)S(1)}, u32[]{:S(2)}, u32[]{:S(2)}) collective-permute-start(bf16[192,640]{1,0:T(8,128)(2,1)S(1)} %copy-done.17), channel_id=1, source_target_pairs={{0,6},{1,7},{2,0},{3,1},{4,2},{5,3},{6,4},{7,5},{8,14},{9,15},{10,... | collective-permute-start | bytes 737288 | tf_op jit(solution)/shard_map/ppermute | solution.py:520
  168.7 9.0 %collective-permute-done.11.refs_3_ = bf16[192,640]{1,0:T(8,128)(2,1)S(1)} collective-permute-done((bf16[192,640]{1,0:T(8,128)(2,1)S(1)}, bf16[192,640]{1,0:T(8,128)(2,1)S(1)}, u32[]{:S(2)}, u32[]{:S(2)}) %collective-permute-start.11) | collective-permute-done | bytes 245792 | tf_op jit(solution)/shard_map/ppermute | solution.py:520
  177.8 3.3 %collective-permute-start.15 = (bf16[192,640]{1,0:T(8,128)(2,1)S(1)}, bf16[192,640]{1,0:T(8,128)(2,1)S(1)}, u32[]{:S(2)}, u32[]{:S(2)}) collective-permute-start(bf16[192,640]{1,0:T(8,128)(2,1)S(1)} %copy-done.16), channel_id=1, source_target_pairs={{0,7},{1,0},{2,1},{3,2},{4,3},{5,4},{6,5},{7,6},{8,15},{9,8},{10,9... | collective-permute-start | bytes 737288 | tf_op jit(solution)/shard_map/ppermute | solution.py:520
  181.1 6.4 %collective-permute-done.12.refs_4_ = bf16[192,640]{1,0:T(8,128)(2,1)S(1)} collective-permute-done((bf16[192,640]{1,0:T(8,128)(2,1)S(1)}, bf16[192,640]{1,0:T(8,128)(2,1)S(1)}, u32[]{:S(2)}, u32[]{:S(2)}) %collective-permute-start.12) | collective-permute-done | bytes 245792 | tf_op jit(solution)/shard_map/ppermute | solution.py:520
  187.5 3.1 %collective-permute-done.14.refs_6_ = bf16[192,640]{1,0:T(8,128)(2,1)S(1)} collective-permute-done((bf16[192,640]{1,0:T(8,128)(2,1)S(1)}, bf16[192,640]{1,0:T(8,128)(2,1)S(1)}, u32[]{:S(2)}, u32[]{:S(2)}) %collective-permute-start.14) | collective-permute-done | bytes 245792 | tf_op jit(solution)/shard_map/ppermute | solution.py:520
  192.9 6.2 %collective-permute-done.9.refs_1_ = bf16[192,640]{1,0:T(8,128)(2,1)S(1)} collective-permute-done((bf16[192,640]{1,0:T(8,128)(2,1)S(1)}, bf16[192,640]{1,0:T(8,128)(2,1)S(1)}, u32[]{:S(2)}, u32[]{:S(2)}) %collective-permute-start.9) | collective-permute-done | bytes 245792 | tf_op jit(solution)/shard_map/ppermute | solution.py:520
  (130 shorter events, 49.4 us)
Async XLA Ops:
  2.7 23.9 %collective-permute-start = (bf16[784,512]{1,0:T(8,128)(2,1)}, bf16[784,512]{1,0:T(8,128)(2,1)S(1)}, u32[]{:S(2)}, u32[]{:S(2)}) collective-permute-start(bf16[784,512]{1,0:T(8,128)(2,1)} %fusion.1), channel_id=1, source_target_pairs={{8,0},{16,8},{24,16},{32,24},{40,32},{48,40},{56,48},{64,56},{72,6... | collective-permute-start | bytes 2408456 | tf_op jit(solution)/shard_map/ppermute | solution.py:455
  5.7 33.9 %all-to-all-start = ((bf16[8,208,256]{2,1,0:T(8,128)(2,1)}), bf16[8,208,256]{2,1,0:T(8,128)(2,1)S(1)}, u32[]{:S(2)}, u32[]{:S(2)}) async-start(bf16[8,208,256]{2,1,0:T(8,128)(2,1)} %shard_map.120), calls=%async_computation | async-start | bytes 1703936 | tf_op jit(solution)/shard_map/all_to_all | solution.py:483
  17.0 25.0 %collective-permute-start.1 = (bf16[192,512]{1,0:T(8,128)(2,1)}, bf16[192,512]{1,0:T(8,128)(2,1)S(1)}, u32[]{:S(2)}, u32[]{:S(2)}) collective-permute-start(bf16[192,512]{1,0:T(8,128)(2,1)} %get-tuple-element.38), channel_id=1, source_target_pairs={{0,1},{1,2},{2,3},{3,4},{4,5},{5,6},{6,7},{7,0},{8,9},{9,10},{10,1... | collective-permute-start | bytes 589832 | tf_op jit(solution)/shard_map/ppermute | solution.py:520
  19.0 32.5 %collective-permute-start.2 = (bf16[192,512]{1,0:T(8,128)(2,1)}, bf16[192,512]{1,0:T(8,128)(2,1)}, u32[]{:S(2)}, u32[]{:S(2)}) collective-permute-start(bf16[192,512]{1,0:T(8,128)(2,1)} %get-tuple-element.39), channel_id=1, source_target_pairs={{0,2},{1,3},{2,4},{3,5},{4,6},{5,7},{6,0},{7,1},{8,10},{9,11},{10,... | collective-permute-start | bytes 589832 | tf_op jit(solution)/shard_map/ppermute | solution.py:520
  21.4 47.1 %collective-permute-start.3 = (bf16[192,512]{1,0:T(8,128)(2,1)}, bf16[192,512]{1,0:T(8,128)(2,1)}, u32[]{:S(2)}, u32[]{:S(2)}) collective-permute-start(bf16[192,512]{1,0:T(8,128)(2,1)} %get-tuple-element.40), channel_id=1, source_target_pairs={{0,3},{1,4},{2,5},{3,6},{4,7},{5,0},{6,1},{7,2},{8,11},{9,12},{10,... | collective-permute-start | bytes 589832 | tf_op jit(solution)/shard_map/ppermute | solution.py:520
  24.1 49.2 %collective-permute-start.4 = (bf16[192,512]{1,0:T(8,128)(2,1)}, bf16[192,512]{1,0:T(8,128)(2,1)}, u32[]{:S(2)}, u32[]{:S(2)}) collective-permute-start(bf16[192,512]{1,0:T(8,128)(2,1)} %get-tuple-element.41), channel_id=1, source_target_pairs={{0,4},{1,5},{2,6},{3,7},{4,0},{5,1},{6,2},{7,3},{8,12},{9,13},{10,... | collective-permute-start | bytes 589832 | tf_op jit(solution)/shard_map/ppermute | solution.py:520
  26.6 46.6 %collective-permute-start.5 = (bf16[192,512]{1,0:T(8,128)(2,1)}, bf16[192,512]{1,0:T(8,128)(2,1)}, u32[]{:S(2)}, u32[]{:S(2)}) collective-permute-start(bf16[192,512]{1,0:T(8,128)(2,1)} %get-tuple-element.42), channel_id=1, source_target_pairs={{0,5},{1,6},{2,7},{3,0},{4,1},{5,2},{6,3},{7,4},{8,13},{9,14},{10,... | collective-permute-start | bytes 589832 | tf_op jit(solution)/shard_map/ppermute | solution.py:520
  42.0 31.2 %collective-permute-start.6 = (bf16[192,512]{1,0:T(8,128)(2,1)}, bf16[192,512]{1,0:T(8,128)(2,1)S(1)}, u32[]{:S(2)}, u32[]{:S(2)}) collective-permute-start(bf16[192,512]{1,0:T(8,128)(2,1)} %get-tuple-element.43), channel_id=1, source_target_pairs={{0,6},{1,7},{2,0},{3,1},{4,2},{5,3},{6,4},{7,5},{8,14},{9,15},{10,... | collective-permute-start | bytes 589832 | tf_op jit(solution)/shard_map/ppermute | solution.py:520
  51.6 21.7 %collective-permute-start.7 = (bf16[192,512]{1,0:T(8,128)(2,1)}, bf16[192,512]{1,0:T(8,128)(2,1)S(1)}, u32[]{:S(2)}, u32[]{:S(2)}) collective-permute-start(bf16[192,512]{1,0:T(8,128)(2,1)} %get-tuple-element.44), channel_id=1, source_target_pairs={{0,7},{1,0},{2,1},{3,2},{4,3},{5,4},{6,5},{7,6},{8,15},{9,8},{10,9... | collective-permute-start | bytes 589832 | tf_op jit(solution)/shard_map/ppermute | solution.py:520
  60.7 20.5 %all-to-all-start.1 = ((f32[32,4,640]{2,1,0:T(4,128)}), f32[32,4,640]{2,1,0:T(4,128)S(1)}, u32[]{:S(2)}, u32[]{:S(2)}) async-start(f32[32,4,640]{2,1,0:T(4,128)} %get-tuple-element.47), calls=%async_computation.1 | async-start | bytes 655360 | tf_op jit(solution)/shard_map/all_to_all | solution.py:486
  81.2 14.9 %all-to-all-start.3 = ((f32[32,4,512]{2,1,0:T(4,128)}), f32[32,4,512]{2,1,0:T(4,128)S(1)}, u32[]{:S(2)}, u32[]{:S(2)}) async-start(f32[32,4,512]{2,1,0:T(4,128)} %get-tuple-element.51), calls=%async_computation.3 | async-start | bytes 524288 | tf_op jit(solution)/shard_map/all_to_all | solution.py:486
  96.1 12.8 %all-to-all-start.2 = ((f32[32,4,512]{2,1,0:T(4,128)}), f32[32,4,512]{2,1,0:T(4,128)S(1)}, u32[]{:S(2)}, u32[]{:S(2)}) async-start(f32[32,4,512]{2,1,0:T(4,128)} %shard_map.125), calls=%async_computation.2 | async-start | bytes 524288 | tf_op jit(solution)/shard_map/all_to_all | solution.py:486
  108.9 16.6 %all-to-all-start.4 = ((f32[32,4,512]{2,1,0:T(4,128)}), f32[32,4,512]{2,1,0:T(4,128)S(1)}, u32[]{:S(2)}, u32[]{:S(2)}) async-start(f32[32,4,512]{2,1,0:T(4,128)} %shard_map.127), calls=%async_computation.4 | async-start | bytes 524288 | tf_op jit(solution)/shard_map/all_to_all | solution.py:486
  126.2 51.6 %copy-start.16 = (bf16[192,640]{1,0:T(8,128)(2,1)S(1)}, bf16[192,640]{1,0:T(8,128)(2,1)}, u32[]{:S(2)}) copy-start(bf16[192,640]{1,0:T(8,128)(2,1)} %get-tuple-element.62) | copy-start | bytes 737284
  126.2 61.2 %copy-start.15 = (bf16[192,640]{1,0:T(8,128)(2,1)S(1)}, bf16[192,640]{1,0:T(8,128)(2,1)}, u32[]{:S(2)}) copy-start(bf16[192,640]{1,0:T(8,128)(2,1)} %get-tuple-element.56) | copy-start | bytes 737284
  133.7 69.7 %collective-permute-start.8 = (bf16[6,128,512]{2,1,0:T(8,128)(2,1)}, bf16[6,128,512]{2,1,0:T(8,128)(2,1)S(1)}, u32[]{:S(2)}, u32[]{:S(2)}) collective-permute-start(bf16[6,128,512]{2,1,0:T(8,128)(2,1)} %get-tuple-element.52), channel_id=1, source_target_pairs={{0,8},{8,16},{16,24},{24,32},{32,40},{40,48},{48,56},{56,64},{64,7... | collective-permute-start | bytes 2359304 | tf_op jit(solution)/shard_map/ppermute | solution.py:455
  135.7 67.0 %all-to-all-start.5 = ((bf16[8,192,128]{2,1,0:T(8,128)(2,1)}), bf16[8,192,128]{2,1,0:T(8,128)(2,1)S(1)}, u32[]{:S(2)}, u32[]{:S(2)}) async-start(bf16[8,192,128]{2,1,0:T(8,128)(2,1)} %bitcast.26), calls=%async_computation.5 | async-start | bytes 786432 | tf_op jit(solution)/shard_map/all_to_all | solution.py:483
  139.2 21.3 %collective-permute-start.10 = (bf16[192,640]{1,0:T(8,128)(2,1)S(1)}, bf16[192,640]{1,0:T(8,128)(2,1)S(1)}, u32[]{:S(2)}, u32[]{:S(2)}) collective-permute-start(bf16[192,640]{1,0:T(8,128)(2,1)S(1)} %copy-done.22), channel_id=1, source_target_pairs={{0,2},{1,3},{2,4},{3,5},{4,6},{5,7},{6,0},{7,1},{8,10},{9,11},{10,... | collective-permute-start | bytes 737288 | tf_op jit(solution)/shard_map/ppermute | solution.py:520
  142.0 35.8 %collective-permute-start.11 = (bf16[192,640]{1,0:T(8,128)(2,1)S(1)}, bf16[192,640]{1,0:T(8,128)(2,1)S(1)}, u32[]{:S(2)}, u32[]{:S(2)}) collective-permute-start(bf16[192,640]{1,0:T(8,128)(2,1)S(1)} %copy-done.20), channel_id=1, source_target_pairs={{0,3},{1,4},{2,5},{3,6},{4,7},{5,0},{6,1},{7,2},{8,11},{9,12},{10,... | collective-permute-start | bytes 737288 | tf_op jit(solution)/shard_map/ppermute | solution.py:520
  145.6 41.8 %collective-permute-start.12 = (bf16[192,640]{1,0:T(8,128)(2,1)S(1)}, bf16[192,640]{1,0:T(8,128)(2,1)S(1)}, u32[]{:S(2)}, u32[]{:S(2)}) collective-permute-start(bf16[192,640]{1,0:T(8,128)(2,1)S(1)} %copy-done.19), channel_id=1, source_target_pairs={{0,4},{1,5},{2,6},{3,7},{4,0},{5,1},{6,2},{7,3},{8,12},{9,13},{10,... | collective-permute-start | bytes 737288 | tf_op jit(solution)/shard_map/ppermute | solution.py:520
  147.0 40.4 %collective-permute-start.13 = (bf16[192,640]{1,0:T(8,128)(2,1)S(1)}, bf16[192,640]{1,0:T(8,128)(2,1)S(1)}, u32[]{:S(2)}, u32[]{:S(2)}) collective-permute-start(bf16[192,640]{1,0:T(8,128)(2,1)S(1)} %copy-done.18), channel_id=1, source_target_pairs={{0,5},{1,6},{2,7},{3,0},{4,1},{5,2},{6,3},{7,4},{8,13},{9,14},{10,... | collective-permute-start | bytes 737288 | tf_op jit(solution)/shard_map/ppermute | solution.py:520
  160.5 30.1 %collective-permute-start.14 = (bf16[192,640]{1,0:T(8,128)(2,1)S(1)}, bf16[192,640]{1,0:T(8,128)(2,1)S(1)}, u32[]{:S(2)}, u32[]{:S(2)}) collective-permute-start(bf16[192,640]{1,0:T(8,128)(2,1)S(1)} %copy-done.17), channel_id=1, source_target_pairs={{0,6},{1,7},{2,0},{3,1},{4,2},{5,3},{6,4},{7,5},{8,14},{9,15},{10,... | collective-permute-start | bytes 737288 | tf_op jit(solution)/shard_map/ppermute | solution.py:520
  177.8 15.1 %collective-permute-start.15 = (bf16[192,640]{1,0:T(8,128)(2,1)S(1)}, bf16[192,640]{1,0:T(8,128)(2,1)S(1)}, u32[]{:S(2)}, u32[]{:S(2)}) collective-permute-start(bf16[192,640]{1,0:T(8,128)(2,1)S(1)} %copy-done.16), channel_id=1, source_target_pairs={{0,7},{1,0},{2,1},{3,2},{4,3},{5,4},{6,5},{7,6},{8,15},{9,8},{10,9... | collective-permute-start | bytes 737288 | tf_op jit(solution)/shard_map/ppermute | solution.py:520
  187.4 11.7 %collective-permute-start.9 = (bf16[192,640]{1,0:T(8,128)(2,1)S(1)}, bf16[192,640]{1,0:T(8,128)(2,1)S(1)}, u32[]{:S(2)}, u32[]{:S(2)}) collective-permute-start(bf16[192,640]{1,0:T(8,128)(2,1)S(1)} %copy-done.15), channel_id=1, source_target_pairs={{0,1},{1,2},{2,3},{3,4},{4,5},{5,6},{6,7},{7,0},{8,9},{9,10},{10,1... | collective-permute-start | bytes 737288 | tf_op jit(solution)/shard_map/ppermute | solution.py:520
  (32 other events, 319.3 us)
